TPU v7x, 512 devices: a whole 4x4x16 slice. The times are simulated.
512 devices in a mesh: section: 16 (over x, z_hi), seq: 16 (over z_lo, y), mp: 2 (over core).
Axes of the slice: x: 4, y: 4, z: 16 (z_hi: 4, z_lo: 4; z = z_hi * 4 + z_lo), core: 2. Of those that a mesh axis runs over, the one named last changes fastest.
Arguments:
- query_rows: bfloat16 [16, 2048, 2048], P('section', 'seq', 'mp'), may hold values from -150 to 150
- key_row_matrix: bfloat16 [16, 2048, 1024], P('section', 'seq', 'mp'), may hold values from -13 to 13
- value_row_matrix: bfloat16 [16, 2048, 1024], P('section', 'seq', 'mp'), may hold values from -6 to 6
- out_grad: bfloat16 [16, 2048, 2048], P('section', 'seq', 'mp'), may hold values from -24 to 24
- w_query: bfloat16 [16, 5376, 2048], P('section', 'seq', 'mp'), may hold values from -0.078125 to 0.078125
- key_weight: bfloat16 [16, 5376, 1024], P('section', 'seq', 'mp'), may hold values from -0.078125 to 0.078125
- value_weight: bfloat16 [16, 5376, 1024], P('section', 'seq', 'mp'), may hold values from -0.078125 to 0.078125
- doc_ids: int32 [16, 2048], P('section'), may hold values from 0 to 5, never falling along the last dimension, each value on 1 to 682 neighbouring positions
Outputs:
- upstream: bfloat16 [16, 2048, 5376], P('section', None, ('seq', 'mp'))
All inputs are finite; a program needn't handle non-finite values.
Results may differ from a plain program's by a relative error of at most 0.0071.
Values may be sent and summed in bfloat16 or wider, within the bound.
A program may use at most 64 MiB of HBM per device.

v0:
```python
from functools import reduce
import math

import jax
import jax.numpy as jnp
from jax import lax
from jax.sharding import PartitionSpec as P

HEAD_WIDTH = 128
WINDOW = 512


def from_behind(shard, axis, by):
    size = lax.axis_size(axis)
    pairs = [(i, i + by) for i in range(size) if 0 <= i + by < size]
    return lax.ppermute(shard, axis, pairs)


def passed_along(block, axis, distance):
    devices = range(lax.axis_size(axis))
    route = [((i - distance) % len(devices), i) for i in devices]
    return lax.ppermute(block, axis, route)


def per_device(
    query_rows,
    key_row_matrix,
    value_row_matrix,
    out_grad,
    w_query,
    key_weight,
    value_weight,
    doc_ids,
):
    query_here = query_rows[0]
    key_here = key_row_matrix[0]
    value_here = value_row_matrix[0]
    grad_here = out_grad[0]
    documents = doc_ids[0]
    row_count = query_here.shape[0]
    kv_cols = key_here.shape[1]
    kv_heads = kv_cols // HEAD_WIDTH
    group_width = query_here.shape[1] // kv_cols
    scaling = 1.0 / math.sqrt(HEAD_WIDTH)
    seq_count = lax.axis_size("seq")
    seq_place = lax.axis_index("seq")
    reach_now = min((WINDOW - 1) // row_count + 1, seq_count - 1)
    kv_local = jnp.concatenate([key_here, value_here], axis=1)
    rim_blocks = [from_behind(kv_local, "seq", distance) for distance in range(reach_now, 0, -1)]
    kv_blocks = rim_blocks + [kv_local]
    block_total = len(kv_blocks)
    span_rows = block_total * row_count
    first_row = seq_place * row_count
    padded_docs = jnp.concatenate([jnp.full((reach_now * row_count,), -1, jnp.int32), documents])
    key_docs = lax.dynamic_slice_in_dim(padded_docs, first_row, span_rows, 0)
    query_docs = lax.dynamic_slice_in_dim(documents, first_row, row_count, 0)
    query_pos = first_row + jnp.arange(row_count, dtype=jnp.int32)
    key_pos = first_row - reach_now * row_count + jnp.arange(span_rows, dtype=jnp.int32)
    offset = query_pos[:, None] - key_pos[None, :]
    allowed = (query_docs[:, None] == key_docs[None, :]) & (offset >= 0) & (offset < WINDOW)
    query_split = query_here.reshape(row_count, kv_heads, group_width, HEAD_WIDTH)
    grad_split = grad_here.reshape(row_count, kv_heads, group_width, HEAD_WIDTH)
    block_masks = [
        allowed[:, block_index * row_count : (block_index + 1) * row_count]
        for block_index in range(block_total)
    ]
    block_keys = [
        kv_block[:, :kv_cols].reshape(row_count, kv_heads, HEAD_WIDTH) for kv_block in kv_blocks
    ]
    block_values = [
        kv_block[:, kv_cols:].reshape(row_count, kv_heads, HEAD_WIDTH) for kv_block in kv_blocks
    ]

    def score_pair(key_block, mask_now):

        def make_fn():
            product = (
                jnp.einsum(
                    "igrd,jgd->grij", query_split, key_block, preferred_element_type=jnp.float32
                )
                * scaling
            )
            return jnp.where(mask_now[None, None], product, -jnp.inf)

        def empty_fn():
            return jnp.full((kv_heads, group_width, row_count, row_count), -jnp.inf, jnp.float32)

        return (make_fn, empty_fn)

    scores = []
    for block_index in range(block_total):
        make_fn, empty_fn = score_pair(block_keys[block_index], block_masks[block_index])
        scores.append(make_fn())
    row_max = reduce(
        jnp.maximum, [jnp.max(score_now, axis=-1, keepdims=True) for score_now in scores]
    )
    raised = [jnp.exp(score_now - row_max) for score_now in scores]
    row_total = reduce(
        jnp.add, [jnp.sum(raised_now, axis=-1, keepdims=True) for raised_now in raised]
    )
    weights_full = [raised_now / row_total for raised_now in raised]
    weights_half = [weight_now.astype(jnp.bfloat16) for weight_now in weights_full]

    def value_pair(weight_half, value_block):

        def make_fn():
            return jnp.einsum(
                "grij,jgd->igrd", weight_half, value_block, preferred_element_type=jnp.float32
            )

        def empty_fn():
            return jnp.zeros((row_count, kv_heads, group_width, HEAD_WIDTH), jnp.float32)

        return (make_fn, empty_fn)

    attended_terms = []
    for block_index in range(block_total):
        make_fn, empty_fn = value_pair(weights_half[block_index], block_values[block_index])
        attended_terms.append(make_fn())
    attended = reduce(jnp.add, attended_terms)
    delta_row = jnp.transpose(
        jnp.sum(grad_split.astype(jnp.float32) * attended, axis=-1), (1, 2, 0)
    )

    def grad_pair(weight_full, weight_half, key_block, value_block):

        def make_fn():
            grad_weights = jnp.einsum(
                "igrd,jgd->grij", grad_split, value_block, preferred_element_type=jnp.float32
            )
            grad_scores = (weight_full * (grad_weights - delta_row[..., None])).astype(jnp.bfloat16)
            query_term = jnp.einsum(
                "grij,jgd->igrd", grad_scores, key_block, preferred_element_type=jnp.float32
            )
            key_term = (
                jnp.einsum(
                    "grij,igrd->jgd", grad_scores, query_split, preferred_element_type=jnp.float32
                )
                * scaling
            )
            value_term = jnp.einsum(
                "grij,igrd->jgd", weight_half, grad_split, preferred_element_type=jnp.float32
            )
            kv_term = jnp.concatenate(
                [key_term.reshape(row_count, kv_cols), value_term.reshape(row_count, kv_cols)],
                axis=1,
            )
            return (query_term, kv_term)

        def empty_fn():
            return (
                jnp.zeros((row_count, kv_heads, group_width, HEAD_WIDTH), jnp.float32),
                jnp.zeros((row_count, 2 * kv_cols), jnp.float32),
            )

        return (make_fn, empty_fn)

    query_terms = []
    kv_terms = []
    for block_index in range(block_total):
        make_fn, empty_fn = grad_pair(
            weights_full[block_index],
            weights_half[block_index],
            block_keys[block_index],
            block_values[block_index],
        )
        query_term, kv_term = make_fn()
        query_terms.append(query_term)
        kv_terms.append(kv_term)
    query_grad = (
        (reduce(jnp.add, query_terms) * scaling)
        .astype(jnp.bfloat16)
        .reshape(row_count, kv_heads * group_width * HEAD_WIDTH)
    )
    kv_total = kv_terms[-1]
    for distance in range(1, reach_now + 1):
        kv_total = kv_total + from_behind(kv_terms[reach_now - distance], "seq", -distance)
    grad_matrix = jnp.concatenate([query_grad, kv_total.astype(jnp.bfloat16)], axis=1)
    weights_all = jnp.concatenate([w_query[0], key_weight[0], value_weight[0]], axis=1)
    partial_grad = lax.dot_general(
        lax.all_gather(grad_matrix, "seq", axis=0, tiled=True),
        weights_all,
        (((1,), (1,)), ((), ())),
        preferred_element_type=jnp.float32,
    )
    summed = lax.psum_scatter(partial_grad, "mp", scatter_dimension=1, tiled=True)
    grad_input = summed.astype(jnp.bfloat16)
    upstream = passed_along(grad_input, "section", -1)
    return upstream[None]


def solution(mesh):
    placed = (
        P("section", "seq", "mp"),
        P("section", "seq", "mp"),
        P("section", "seq", "mp"),
        P("section", "seq", "mp"),
        P("section", "seq", "mp"),
        P("section", "seq", "mp"),
        P("section", "seq", "mp"),
        P("section", None),
    )
    return jax.shard_map(
        per_device,
        mesh=mesh,
        in_specs=placed,
        out_specs=P("section", None, ("seq", "mp")),
        check_vma=False,
    )
```

profile of v0, /device:TPU:1, one launch (start us, length us, event | category | flops | bytes accessed | tf_op | source)
XLA Modules:
  0.0 335.6 jit_solution(13602698483485576235)
XLA Ops:
  6.5 1.1 copy.60
  7.6 1.0 copy.61
  8.7 4.0 %collective-permute-start.3 = (bf16[128,1024]{0,1:T(8,128)(2,1)S(1)}, bf16[128,1024]{0,1:T(8,128)(2,1)S(1)}, u32[]{:S(2)}, u32[]{:S(2)}) collective-permute-start(bf16[128,1024]{0,1:T(8,128)(2,1)S(1)} %pad_maximum_fusion.5), channel_id=1, source_target_pairs={{0,2},{2,4},{4,6},{6,8},{8,10},{10,12},{12,14},{14,16},{16,18},{18... | collective-permute-start | bytes 786440 | tf_op jit(solution)/shard_map/ppermute | solution.py:16
  12.7 4.5 %collective-permute-start.2 = (bf16[128,1024]{0,1:T(8,128)(2,1)S(1)}, bf16[128,1024]{0,1:T(8,128)(2,1)S(1)}, u32[]{:S(2)}, u32[]{:S(2)}) collective-permute-start(bf16[128,1024]{0,1:T(8,128)(2,1)S(1)} %pad_maximum_fusion.5), channel_id=1, source_target_pairs={{0,4},{2,6},{4,8},{6,10},{8,12},{10,14},{12,16},{14,18},{16,20},{1... | collective-permute-start | bytes 786440 | tf_op jit(solution)/shard_map/ppermute | solution.py:16
  17.3 4.3 %collective-permute-start.1 = (bf16[128,1024]{0,1:T(8,128)(2,1)S(1)}, bf16[128,1024]{0,1:T(8,128)(2,1)S(1)}, u32[]{:S(2)}, u32[]{:S(2)}) collective-permute-start(bf16[128,1024]{0,1:T(8,128)(2,1)S(1)} %pad_maximum_fusion.5), channel_id=1, source_target_pairs={{0,6},{2,8},{4,10},{6,12},{8,14},{10,16},{12,18},{14,20},{16,22},{... | collective-permute-start | bytes 786440 | tf_op jit(solution)/shard_map/ppermute | solution.py:16
  21.6 3.5 %collective-permute-start = (bf16[128,1024]{0,1:T(8,128)(2,1)S(1)}, bf16[128,1024]{0,1:T(8,128)(2,1)S(1)}, u32[]{:S(2)}, u32[]{:S(2)}) collective-permute-start(bf16[128,1024]{0,1:T(8,128)(2,1)S(1)} %pad_maximum_fusion.5), channel_id=1, source_target_pairs={{0,8},{2,10},{4,12},{6,14},{8,16},{10,18},{12,20},{14,22},{16,24},... | collective-permute-start | bytes 786440 | tf_op jit(solution)/shard_map/ppermute | solution.py:16
  25.2 0.7 dynamic-slice_bitcast_fusion
  25.8 0.8 pad_dynamic-slice_fusion
  26.6 0.2 fusion.63
  26.9 0.9 reshape_squeeze.13
  27.8 0.9 reshape_squeeze.15
  28.9 1.1 copy.189
  30.2 0.3 fusion.77
  30.5 0.3 fusion.80
  30.9 0.3 fusion.81
  31.2 0.3 fusion.79
  31.5 0.3 fusion.78
  31.9 0.5 fusion.55
  32.4 0.5 fusion.67
  32.8 0.2 fusion.91
  34.4 0.3 convolution_bitcast_fusion.1
  34.7 0.3 fusion.42
  35.0 0.3 fusion.39
  35.2 0.3 fusion.38
  35.5 0.3 fusion.37
  35.8 0.2 fusion.36
  36.1 0.3 fusion.40
  36.3 0.2 fusion.92
  36.6 0.2 fusion.44
  37.0 0.2 fusion.46
  37.5 0.2 fusion.45
  37.9 0.2 fusion.47
  38.4 1.3 collective-permute-start.5
  39.8 1.3 collective-permute-start.6
  41.1 1.3 collective-permute-start.4
  42.5 1.3 collective-permute-start.7
  43.8 0.2 fusion.43
  44.0 0.3 fusion.41
  44.3 25.0 %collective-permute-done.5 = f32[128,1024]{0,1:T(8,128)S(1)} collective-permute-done((f32[128,1024]{0,1:T(8,128)S(1)}, f32[128,1024]{0,1:T(8,128)S(1)}, u32[]{:S(2)}, u32[]{:S(2)}) %collective-permute-start.5) | collective-permute-done | bytes 524320 | tf_op jit(solution)/shard_map/ppermute | solution.py:16
  69.3 23.3 %collective-permute-done.7 = f32[128,1024]{0,1:T(8,128)S(1)} collective-permute-done((f32[128,1024]{0,1:T(8,128)S(1)}, f32[128,1024]{0,1:T(8,128)S(1)}, u32[]{:S(2)}, u32[]{:S(2)}) %collective-permute-start.7) | collective-permute-done | bytes 524320 | tf_op jit(solution)/shard_map/ppermute | solution.py:16
  92.8 0.8 pad_maximum_fusion.4
  93.7 126.9 %all-gather.2.cloned.1.call-done = bf16[2048,2048]{0,1:T(8,128)(2,1)} async-done(((bf16[128,2048]{0,1:T(8,128)(2,1)}), bf16[2048,2048]{0,1:T(8,128)(2,1)}) %all-gather.2.cloned.1.call-update) | async-done | bytes 8388624 | tf_op jit(solution)/shard_map/all_gather | solution.py:181
  220.6 8.0 %fusion = f32[2048,336]{0,1:T(8,128)} fusion(bf16[2048,2048]{0,1:T(8,128)(2,1)} %all-gather.2.cloned.1.call-done, bf16[336,512]{1,0:T(8,128)(2,1)S(1)} %bitcast.386, bf16[336,512]{1,0:T(8,128)(2,1)S(1)} %bitcast.387, bf16[336,1024]{1,0:T(8,128)(2,1)S(1)} %bitcast.385), kind=kOutput, calls=%fused_computation | convolution fusion | flops 2822701056 | bytes 12517376 | tf_op jit(solution)/shard_map/dot_general | solution.py:180
  228.7 30.3 %reduce-scatter.2.cloned.1.call-done = f32[2048,168]{0,1:T(8,128)} async-done(((f32[2048,336]{0,1:T(8,128)}), f32[2048,168]{0,1:T(8,128)}) %reduce-scatter.2.cloned.1.call-update) | async-done | bytes 1376272 | tf_op jit(solution)/shard_map/reduce_scatter | solution.py:186
  259.0 1.4 convert_element_type.55
  260.4 9.5 %collective-permute-start.8 = (bf16[2048,168]{0,1:T(8,128)(2,1)S(1)}, bf16[2048,168]{0,1:T(8,128)(2,1)S(1)}, u32[]{:S(2)}, u32[]{:S(2)}) collective-permute-start(bf16[2048,168]{0,1:T(8,128)(2,1)S(1)} %convert_element_type.55), channel_id=1, source_target_pairs={{32,0},{64,32},{96,64},{128,96},{160,128},{192,160},{224,192},{256... | collective-permute-start | bytes 2064392 | tf_op jit(solution)/shard_map/ppermute | solution.py:22
  269.9 58.0 %collective-permute-done.8 = bf16[2048,168]{0,1:T(8,128)(2,1)S(1)} collective-permute-done((bf16[2048,168]{0,1:T(8,128)(2,1)S(1)}, bf16[2048,168]{0,1:T(8,128)(2,1)S(1)}, u32[]{:S(2)}, u32[]{:S(2)}) %collective-permute-start.8) | collective-permute-done | bytes 688160 | tf_op jit(solution)/shard_map/ppermute | solution.py:22
  327.9 0.8 copy.195
  (44 shorter events, 3.0 us)
Async XLA Ops:
  6.5 23.5 %copy-start = (bf16[1,128,1024]{2,1,0:T(8,128)(2,1)S(1)}, bf16[1,128,1024]{2,1,0:T(8,128)(2,1)}, u32[]{:S(2)}) copy-start(bf16[1,128,1024]{2,1,0:T(8,128)(2,1)} %param.11) | copy-start | bytes 786436
  6.5 214.1 %all-gather.2.cloned.1.call-start = ((), (), s32[]{:S(2)}) async-start(), calls=%async_computation.1 | async-start | bytes 8912896 | tf_op jit(solution)/shard_map/all_gather | solution.py:181
  8.7 22.8 %collective-permute-start.3 = (bf16[128,1024]{0,1:T(8,128)(2,1)S(1)}, bf16[128,1024]{0,1:T(8,128)(2,1)S(1)}, u32[]{:S(2)}, u32[]{:S(2)}) collective-permute-start(bf16[128,1024]{0,1:T(8,128)(2,1)S(1)} %pad_maximum_fusion.5), channel_id=1, source_target_pairs={{0,2},{2,4},{4,6},{6,8},{8,10},{10,12},{12,14},{14,16},{16,18},{18... | collective-permute-start | bytes 786440 | tf_op jit(solution)/shard_map/ppermute | solution.py:16
  12.7 18.4 %collective-permute-start.2 = (bf16[128,1024]{0,1:T(8,128)(2,1)S(1)}, bf16[128,1024]{0,1:T(8,128)(2,1)S(1)}, u32[]{:S(2)}, u32[]{:S(2)}) collective-permute-start(bf16[128,1024]{0,1:T(8,128)(2,1)S(1)} %pad_maximum_fusion.5), channel_id=1, source_target_pairs={{0,4},{2,6},{4,8},{6,10},{8,12},{10,14},{12,16},{14,18},{16,20},{1... | collective-permute-start | bytes 786440 | tf_op jit(solution)/shard_map/ppermute | solution.py:16
  17.3 13.6 %collective-permute-start.1 = (bf16[128,1024]{0,1:T(8,128)(2,1)S(1)}, bf16[128,1024]{0,1:T(8,128)(2,1)S(1)}, u32[]{:S(2)}, u32[]{:S(2)}) collective-permute-start(bf16[128,1024]{0,1:T(8,128)(2,1)S(1)} %pad_maximum_fusion.5), channel_id=1, source_target_pairs={{0,6},{2,8},{4,10},{6,12},{8,14},{10,16},{12,18},{14,20},{16,22},{... | collective-permute-start | bytes 786440 | tf_op jit(solution)/shard_map/ppermute | solution.py:16
  21.6 8.9 %collective-permute-start = (bf16[128,1024]{0,1:T(8,128)(2,1)S(1)}, bf16[128,1024]{0,1:T(8,128)(2,1)S(1)}, u32[]{:S(2)}, u32[]{:S(2)}) collective-permute-start(bf16[128,1024]{0,1:T(8,128)(2,1)S(1)} %pad_maximum_fusion.5), channel_id=1, source_target_pairs={{0,8},{2,10},{4,12},{6,14},{8,16},{10,18},{12,20},{14,22},{16,24},... | collective-permute-start | bytes 786440 | tf_op jit(solution)/shard_map/ppermute | solution.py:16
  38.4 30.9 %collective-permute-start.5 = (f32[128,1024]{0,1:T(8,128)S(1)}, f32[128,1024]{0,1:T(8,128)S(1)}, u32[]{:S(2)}, u32[]{:S(2)}) collective-permute-start(f32[128,1024]{0,1:T(8,128)S(1)} %pad_maximum_fusion.1), channel_id=1, source_target_pairs={{4,0},{6,2},{8,4},{10,6},{12,8},{14,10},{16,12},{18,14},{20,16},{2... | collective-permute-start | bytes 1572872 | tf_op jit(solution)/shard_map/ppermute | solution.py:16
  39.8 29.6 %collective-permute-start.6 = (f32[128,1024]{0,1:T(8,128)S(1)}, f32[128,1024]{0,1:T(8,128)S(1)}, u32[]{:S(2)}, u32[]{:S(2)}) collective-permute-start(f32[128,1024]{0,1:T(8,128)S(1)} %pad_maximum_fusion.2), channel_id=1, source_target_pairs={{6,0},{8,2},{10,4},{12,6},{14,8},{16,10},{18,12},{20,14},{22,16},{... | collective-permute-start | bytes 1572872 | tf_op jit(solution)/shard_map/ppermute | solution.py:16
  41.1 28.2 %collective-permute-start.4 = (f32[128,1024]{0,1:T(8,128)S(1)}, f32[128,1024]{0,1:T(8,128)S(1)}, u32[]{:S(2)}, u32[]{:S(2)}) collective-permute-start(f32[128,1024]{0,1:T(8,128)S(1)} %pad_maximum_fusion), channel_id=1, source_target_pairs={{2,0},{4,2},{6,4},{8,6},{10,8},{12,10},{14,12},{16,14},{18,16},{20... | collective-permute-start | bytes 1572872 | tf_op jit(solution)/shard_map/ppermute | solution.py:16
  42.5 50.2 %collective-permute-start.7 = (f32[128,1024]{0,1:T(8,128)S(1)}, f32[128,1024]{0,1:T(8,128)S(1)}, u32[]{:S(2)}, u32[]{:S(2)}) collective-permute-start(f32[128,1024]{0,1:T(8,128)S(1)} %pad_maximum_fusion.3), channel_id=1, source_target_pairs={{8,0},{10,2},{12,4},{14,6},{16,8},{18,10},{20,12},{22,14},{24,16},... | collective-permute-start | bytes 1572872 | tf_op jit(solution)/shard_map/ppermute | solution.py:16
  44.3 176.4 %copy-start.1 = (bf16[1,336,1024]{2,1,0:T(8,128)(2,1)S(1)}, bf16[1,336,1024]{2,1,0:T(8,128)(2,1)}, u32[]{:S(2)}) copy-start(bf16[1,336,1024]{2,1,0:T(8,128)(2,1)} %param.12) | copy-start | bytes 2064388
  44.3 176.3 %copy-start.2 = (bf16[1,336,512]{2,1,0:T(8,128)(2,1)S(1)}, bf16[1,336,512]{2,1,0:T(8,128)(2,1)}, u32[]{:S(2)}) copy-start(bf16[1,336,512]{2,1,0:T(8,128)(2,1)} %param.14) | copy-start | bytes 1032196
  44.3 176.3 %copy-start.3 = (bf16[1,336,512]{2,1,0:T(8,128)(2,1)S(1)}, bf16[1,336,512]{2,1,0:T(8,128)(2,1)}, u32[]{:S(2)}) copy-start(bf16[1,336,512]{2,1,0:T(8,128)(2,1)} %param.13) | copy-start | bytes 1032196
  93.6 165.4 %reduce-scatter.2.cloned.1.call-start = ((), (), s32[]{:S(2)}) async-start(), calls=%async_computation.2 | async-start | bytes 4128768 | tf_op jit(solution)/shard_map/reduce_scatter | solution.py:186
  260.4 67.5 %collective-permute-start.8 = (bf16[2048,168]{0,1:T(8,128)(2,1)S(1)}, bf16[2048,168]{0,1:T(8,128)(2,1)S(1)}, u32[]{:S(2)}, u32[]{:S(2)}) collective-permute-start(bf16[2048,168]{0,1:T(8,128)(2,1)S(1)} %convert_element_type.55), channel_id=1, source_target_pairs={{32,0},{64,32},{96,64},{128,96},{160,128},{192,160},{224,192},{256... | collective-permute-start | bytes 2064392 | tf_op jit(solution)/shard_map/ppermute | solution.py:22
Sparse Core Ops, SparseCore 0:
  93.7 126.8 all-gather.1
  228.8 30.1 reduce-scatter.1
where the time goes:
time: 337 us; the launch traced here: 336 us
  waiting for transfers between devices  264 us (78%)
  starting transfers between devices  31.2 us (9%)
  matrix products  15.4 us (5%)
  between operations  13.9 us (4%)
  local copies, waits for them, and re-layouts  7.01 us (2%)
  other arithmetic  4.5 us (1%)
    all_gather x1, waiting for transfers between devices, per_device(): lax.all_gather(grad_matrix, 'seq', axis=0, tiled=True)  127 us
    ppermute x1, waiting for transfers between devices, passed_along(): return lax.ppermute(block, axis, route)  58 us
    ppermute x8, waiting for transfers between devices, from_behind(): return lax.ppermute(shard, axis, pairs)  48.4 us
    reduce_scatter x1, waiting for transfers between devices, per_device(): lax.psum_scatter(partial_grad, 'mp', scatter_dimension=1, tiled=True)  30.3 us
    ppermute x8, starting transfers between devices, from_behind(): return lax.ppermute(shard, axis, pairs)  21.6 us
    ppermute x1, starting transfers between devices, passed_along(): return lax.ppermute(block, axis, route)  9.49 us
    dot_general x1, matrix products, per_device(): lax.dot_general(lax.all_gather(grad_matrix, 'seq', axis=0, tiled=True), w...  8.02 us
  transfers between devices with their start and end apart: 11, of which 5 were waited for; matrix products, arithmetic and copies ran while one was open for 2% of the time, Pallas kernels for 0%

commit v1 on v0

--- a/solution.py
+++ b/solution.py
@@ -4,10 +4,14 @@
 import jax
 import jax.numpy as jnp
 from jax import lax
+from jax.experimental import pallas as pl
+from jax.experimental.pallas import tpu as pltpu
 from jax.sharding import PartitionSpec as P
 
 HEAD_WIDTH = 128
 WINDOW = 512
+RING = 4
+MESH = pl.DeviceIdType.MESH
 
 
 def from_behind(shard, axis, by):
@@ -16,10 +20,275 @@
     return lax.ppermute(shard, axis, pairs)
 
 
-def passed_along(block, axis, distance):
-    devices = range(lax.axis_size(axis))
-    route = [((i - distance) % len(devices), i) for i in devices]
-    return lax.ppermute(block, axis, route)
+NT = (((1,), (1,)), ((), ()))
+
+
+def spread_kernel(
+    grad_query_ref,
+    grad_kv_ref,
+    w_query_ref,
+    key_weight_ref,
+    value_weight_ref,
+    out_ref,
+    held,
+    part,
+    part_in,
+    ready,
+    landed,
+    own_sem,
+    up_send,
+    up_recv,
+    down_send,
+    down_recv,
+    right_send,
+    right_recv,
+    left_send,
+    left_recv,
+    far_right_send,
+    far_right_recv,
+    far_left_send,
+    far_left_recv,
+    core_send,
+    core_recv,
+    section_send,
+    section_recv,
+):
+    seq_place = lax.axis_index("seq")
+    core = lax.axis_index("mp")
+    section = lax.axis_index("section")
+    section_count = lax.axis_size("section")
+    run = seq_place // RING
+    turn = lax.rem(seq_place, RING)
+    right = run * RING + lax.rem(turn + 1, RING)
+    left = run * RING + lax.rem(turn + RING - 1, RING)
+    back_section = lax.rem(section + section_count - 1, section_count)
+    next_section = lax.rem(section + 1, section_count)
+    rows = held.shape[2]
+    half = rows // 2
+    kv_cols = key_weight_ref.shape[1]
+    width = w_query_ref.shape[0] // 2
+
+    barrier = pltpu.get_barrier_semaphore()
+    for place in (right, left):
+        pl.semaphore_signal(barrier, inc=1, device_id={"seq": place}, device_id_type=MESH)
+    pl.semaphore_signal(barrier, inc=1, device_id={"mp": 1 - core}, device_id_type=MESH)
+    pl.semaphore_signal(barrier, inc=1, device_id={"section": back_section}, device_id_type=MESH)
+    pl.semaphore_signal(barrier, inc=1, device_id={"section": next_section}, device_id_type=MESH)
+
+    @pl.when(run < RING - 1)
+    def _():
+        pl.semaphore_signal(barrier, inc=1, device_id={"seq": seq_place + RING}, device_id_type=MESH)
+
+    @pl.when(run > 0)
+    def _():
+        pl.semaphore_signal(barrier, inc=1, device_id={"seq": seq_place - RING}, device_id_type=MESH)
+
+    in_line = (run > 0).astype(jnp.int32) + (run < RING - 1).astype(jnp.int32)
+    pl.semaphore_wait(barrier, 5 + in_line)
+
+    def own_copy(piece):
+        source = grad_query_ref if piece == 0 else grad_kv_ref
+        return pltpu.make_async_copy(source, held.at[piece, seq_place], own_sem.at[piece])
+
+    def shard_copy(piece, owner, to, send, recv, line):
+        block = held.at[piece, owner]
+        return pltpu.make_async_remote_copy(
+            src_ref=block,
+            dst_ref=block,
+            send_sem=send.at[piece, line],
+            recv_sem=recv.at[piece, line],
+            device_id={"seq": to},
+            device_id_type=MESH,
+        )
+
+    def half_copy(piece, owner, start, to, send, recv, line):
+        block = held.at[piece, owner, pl.ds(start, half)]
+        return pltpu.make_async_remote_copy(
+            src_ref=block,
+            dst_ref=block,
+            send_sem=send.at[piece, line],
+            recv_sem=recv.at[piece, line],
+            device_id={"seq": to},
+            device_id_type=MESH,
+        )
+
+    def column(line, step):
+        return line * RING + lax.rem(turn + step + RING, RING)
+
+    def up_copy(piece, line):
+        return shard_copy(piece, column(line, 0), seq_place + RING, up_send, up_recv, line)
+
+    def down_copy(piece, line):
+        return shard_copy(piece, column(line, 0), seq_place - RING, down_send, down_recv, line)
+
+    def right_copy(piece, line, step=0):
+        return shard_copy(piece, column(line, step), right, right_send, right_recv, line)
+
+    def left_copy(piece, line, step=0):
+        return shard_copy(piece, column(line, step), left, left_send, left_recv, line)
+
+    def far_right_copy(piece, line, step=-1):
+        return half_copy(piece, column(line, step), 0, right, far_right_send, far_right_recv, line)
+
+    def far_left_copy(piece, line, step=1):
+        return half_copy(piece, column(line, step), half, left, far_left_send, far_left_recv, line)
+
+    def along_ring(piece, line):
+        right_copy(piece, line).start()
+        left_copy(piece, line).start()
+
+    def from_line(piece, line):
+        @pl.when(line < run)
+        def _():
+            up_copy(piece, line).wait_recv()
+
+            @pl.when(run < RING - 1)
+            def _():
+                up_copy(piece, line).start()
+
+        @pl.when(line > run)
+        def _():
+            down_copy(piece, line).wait_recv()
+
+            @pl.when(run > 0)
+            def _():
+                down_copy(piece, line).start()
+
+        along_ring(piece, line)
+
+    def farther(piece, line):
+        right_copy(piece, line, -1).wait_recv()
+        far_right_copy(piece, line).start()
+        left_copy(piece, line, 1).wait_recv()
+        far_left_copy(piece, line).start()
+
+    def last_of(piece, line):
+        far_right_copy(piece, line, -2).wait_recv()
+        far_left_copy(piece, line, 2).wait_recv()
+
+    def core_copy(line):
+        return pltpu.make_async_remote_copy(
+            src_ref=part.at[line, 1 - core],
+            dst_ref=part_in.at[line],
+            send_sem=core_send.at[line],
+            recv_sem=core_recv.at[line],
+            device_id={"mp": 1 - core},
+            device_id_type=MESH,
+        )
+
+    def section_copy(line):
+        return pltpu.make_async_remote_copy(
+            src_ref=ready.at[line],
+            dst_ref=landed.at[line],
+            send_sem=section_send.at[line],
+            recv_sem=section_recv.at[line],
+            device_id={"section": back_section},
+            device_id_type=MESH,
+        )
+
+    def project(line):
+        base = line * RING
+        query_rows = held[0, pl.ds(base, RING)].reshape(RING * rows, -1)
+        kv_rows = held[1, pl.ds(base, RING)].reshape(RING * rows, -1)
+        product = lax.dot_general(
+            w_query_ref[...], query_rows, NT, preferred_element_type=jnp.float32
+        )
+        product += lax.dot_general(
+            key_weight_ref[...], kv_rows[:, :kv_cols], NT, preferred_element_type=jnp.float32
+        )
+        product += lax.dot_general(
+            value_weight_ref[...], kv_rows[:, kv_cols:], NT, preferred_element_type=jnp.float32
+        )
+        part[line, 0] = product[:width]
+        part[line, 1] = product[width:]
+        core_copy(line).start()
+
+    def hand_over(line):
+        core_copy(line).wait_recv()
+        ready[line] = (part[line, core] + part_in[line]).astype(jnp.bfloat16)
+        section_copy(line).start()
+
+    lines = [
+        run,
+        jnp.where(run == 0, 1, run - 1),
+        jnp.where(run == 0, 2, jnp.where(run == 3, 1, run + 1)),
+        jnp.where(run < 2, 3, 0),
+    ]
+    pieces = (0, 1)
+    for piece in pieces:
+        own_copy(piece).start()
+    for piece in pieces:
+        own_copy(piece).wait()
+
+        @pl.when(run < RING - 1)
+        def _():
+            up_copy(piece, run).start()
+
+        @pl.when(run > 0)
+        def _():
+            down_copy(piece, run).start()
+
+        along_ring(piece, run)
+    for order in range(1, RING + 2):
+        if order < RING:
+            for piece in pieces:
+                from_line(piece, lines[order])
+        if order <= RING:
+            for piece in pieces:
+                farther(piece, lines[order - 1])
+        if order >= 2:
+            for piece in pieces:
+                last_of(piece, lines[order - 2])
+            project(lines[order - 2])
+            hand_over(lines[order - 2])
+    for line in range(RING):
+        section_copy(line).wait_recv()
+        out_ref[line] = landed[line]
+    for line in range(RING):
+        core_copy(line).wait_send()
+        section_copy(line).wait_send()
+        for piece in pieces:
+            right_copy(piece, line).wait_send()
+            left_copy(piece, line).wait_send()
+            far_right_copy(piece, line).wait_send()
+            far_left_copy(piece, line).wait_send()
+
+            @pl.when((run < RING - 1) & (line <= run))
+            def _():
+                up_copy(piece, line).wait_send()
+
+            @pl.when((run > 0) & (line >= run))
+            def _():
+                down_copy(piece, line).wait_send()
+
+
+def spread_and_project(grad_query, grad_kv, w_query, key_weight, value_weight):
+    rows = grad_query.shape[0]
+    cols = grad_query.shape[1]
+    seq_count = lax.axis_size("seq")
+    width = w_query.shape[0] // 2
+    span = RING * rows
+    dma = pltpu.SemaphoreType.DMA
+    pairs = [dma((2, RING))] * 12
+    whole = pl.BlockSpec(memory_space=pltpu.VMEM)
+    out = pl.pallas_call(
+        spread_kernel,
+        out_shape=jax.ShapeDtypeStruct((RING, width, span), jnp.bfloat16),
+        in_specs=[whole] * 5,
+        out_specs=whole,
+        scratch_shapes=[
+            pltpu.VMEM((2, seq_count, rows, cols), jnp.bfloat16),
+            pltpu.VMEM((RING, 2, width, span), jnp.float32),
+            pltpu.VMEM((RING, width, span), jnp.float32),
+            pltpu.VMEM((RING, width, span), jnp.bfloat16),
+            pltpu.VMEM((RING, width, span), jnp.bfloat16),
+            dma((2,)),
+            *pairs,
+            *([dma((RING,))] * 4),
+        ],
+        compiler_params=pltpu.CompilerParams(collective_id=0, has_side_effects=True),
+    )(grad_query, grad_kv, w_query, key_weight, value_weight)
+    return jnp.transpose(out, (0, 2, 1)).reshape(seq_count * rows, width)
 
 
 def per_device(
@@ -175,17 +444,8 @@
     kv_total = kv_terms[-1]
     for distance in range(1, reach_now + 1):
         kv_total = kv_total + from_behind(kv_terms[reach_now - distance], "seq", -distance)
-    grad_matrix = jnp.concatenate([query_grad, kv_total.astype(jnp.bfloat16)], axis=1)
-    weights_all = jnp.concatenate([w_query[0], key_weight[0], value_weight[0]], axis=1)
-    partial_grad = lax.dot_general(
-        lax.all_gather(grad_matrix, "seq", axis=0, tiled=True),
-        weights_all,
-        (((1,), (1,)), ((), ())),
-        preferred_element_type=jnp.float32,
-    )
-    summed = lax.psum_scatter(partial_grad, "mp", scatter_dimension=1, tiled=True)
-    grad_input = summed.astype(jnp.bfloat16)
-    upstream = passed_along(grad_input, "section", -1)
+    kv_half = kv_total.astype(jnp.bfloat16)
+    upstream = spread_and_project(query_grad, kv_half, w_query[0], key_weight[0], value_weight[0])
     return upstream[None]
 
 

time: 337 us -> 226 us (0.67)
  waiting for transfers between devices: 264 us -> 39.9 us
  Pallas kernels: 0 us -> 125 us
  between operations: 13.9 us -> 0.5 us
  local copies, waits for them, and re-layouts: 7.01 us -> 16.8 us
  starting transfers between devices: 31.2 us -> 21.6 us
  other arithmetic: 4.5 us -> 10 us
  matrix products: 15.4 us -> 10.9 us
    all_gather x1 -> x0, waiting for transfers between devices: 127 us -> none  [per_device(): lax.all_gather(grad_matrix, 'seq', axis=0, tiled=True)]
    pallas_call x0 -> x1, Pallas kernels: none -> 125 us  [spread_and_project(): pl.pallas_call(spread_kernel, out_shape=jax.ShapeDtypeStruct((RING, width...]
    ppermute x1 -> x0, waiting for transfers between devices: 58 us -> none  [passed_along(): return lax.ppermute(block, axis, route)]
    reduce_scatter x1 -> x0, waiting for transfers between devices: 30.3 us -> none  [per_device(): lax.psum_scatter(partial_grad, 'mp', scatter_dimension=1, tiled=True)]
    ppermute x1 -> x0, starting transfers between devices: 9.49 us -> none  [passed_along(): return lax.ppermute(block, axis, route)]
    ppermute x8, waiting for transfers between devices: 48.4 us -> 39.9 us  [from_behind(): return lax.ppermute(shard, axis, pairs)]
    reshape x0 -> x11, local copies, waits for them, and re-layouts: none -> 8.38 us  [the longest x5 4.73 us: make_fn(): key_term.reshape(row_count, kv_cols)]
    dot_general x1 -> x0, matrix products: 8.02 us -> none  [per_device(): lax.dot_general(lax.all_gather(grad_matrix, 'seq', axis=0, tiled=True), w...]
  transfers between devices with their start and end apart: 11 -> 8, of which waited for: 5 -> 3; matrix products, arithmetic and copies ran while one was open for 2% -> 6% of each run, Pallas kernels for 0% -> 0%
where the time goes in v1:
time: 226 us; the launch traced here: 225 us
  Pallas kernels  125 us (55%)
  waiting for transfers between devices  39.9 us (18%)
  starting transfers between devices  21.6 us (10%)
  local copies, waits for them, and re-layouts  16.8 us (7%)
  matrix products  10.9 us (5%)
  other arithmetic  10 us (4%)
    pallas_call x1, Pallas kernels, spread_and_project(): pl.pallas_call(spread_kernel, out_shape=jax.ShapeDtypeStruct((RING, width...  125 us
    ppermute x8, waiting for transfers between devices, from_behind(): return lax.ppermute(shard, axis, pairs)  39.9 us
    ppermute x8, starting transfers between devices, from_behind(): return lax.ppermute(shard, axis, pairs)  21.6 us
    concatenate x4, other arithmetic, make_fn(): jnp.concatenate([key_term.reshape(row_count, kv_cols), value_term.reshape...  6.47 us
    unnamed x23, local copies, waits for them, and re-layouts  5.2 us
    reshape x5, local copies, waits for them, and re-layouts, make_fn(): key_term.reshape(row_count, kv_cols)  4.73 us
  transfers between devices with their start and end apart: 8, of which 3 were waited for; matrix products, arithmetic and copies ran while one was open for 6% of the time, Pallas kernels for 0%

profile of v1, /device:TPU:1, one launch (start us, length us, event | category | flops | bytes accessed | tf_op | source)
XLA Modules:
  0.0 225.0 jit_solution(16405799814791104724)
XLA Ops:
  0.0 1.1 copy.71
  1.2 4.0 %collective-permute-start.3 = (bf16[128,1024]{0,1:T(8,128)(2,1)S(1)}, bf16[128,1024]{0,1:T(8,128)(2,1)S(1)}, u32[]{:S(2)}, u32[]{:S(2)}) collective-permute-start(bf16[128,1024]{0,1:T(8,128)(2,1)S(1)} %pad_maximum_fusion.4), channel_id=1, source_target_pairs={{0,2},{2,4},{4,6},{6,8},{8,10},{10,12},{12,14},{14,16},{16,18},{18... | collective-permute-start | bytes 786440 | tf_op jit(solution)/shard_map/ppermute | solution.py:20
  5.3 4.5 %collective-permute-start.2 = (bf16[128,1024]{0,1:T(8,128)(2,1)S(1)}, bf16[128,1024]{0,1:T(8,128)(2,1)S(1)}, u32[]{:S(2)}, u32[]{:S(2)}) collective-permute-start(bf16[128,1024]{0,1:T(8,128)(2,1)S(1)} %pad_maximum_fusion.4), channel_id=1, source_target_pairs={{0,4},{2,6},{4,8},{6,10},{8,12},{10,14},{12,16},{14,18},{16,20},{1... | collective-permute-start | bytes 786440 | tf_op jit(solution)/shard_map/ppermute | solution.py:20
  9.8 3.5 %collective-permute-start = (bf16[128,1024]{0,1:T(8,128)(2,1)S(1)}, bf16[128,1024]{0,1:T(8,128)(2,1)S(1)}, u32[]{:S(2)}, u32[]{:S(2)}) collective-permute-start(bf16[128,1024]{0,1:T(8,128)(2,1)S(1)} %pad_maximum_fusion.4), channel_id=1, source_target_pairs={{0,8},{2,10},{4,12},{6,14},{8,16},{10,18},{12,20},{14,22},{16,24},... | collective-permute-start | bytes 786440 | tf_op jit(solution)/shard_map/ppermute | solution.py:20
  13.4 4.3 %collective-permute-start.1 = (bf16[128,1024]{0,1:T(8,128)(2,1)S(1)}, bf16[128,1024]{0,1:T(8,128)(2,1)S(1)}, u32[]{:S(2)}, u32[]{:S(2)}) collective-permute-start(bf16[128,1024]{0,1:T(8,128)(2,1)S(1)} %pad_maximum_fusion.4), channel_id=1, source_target_pairs={{0,6},{2,8},{4,10},{6,12},{8,14},{10,16},{12,18},{14,20},{16,22},{... | collective-permute-start | bytes 786440 | tf_op jit(solution)/shard_map/ppermute | solution.py:20
  17.7 0.7 copy-done.9
  18.8 0.6 copy-done.5
  19.5 0.9 copy-done.7
  20.7 0.8 copy-done.8
  21.7 0.3 fusion.70
  22.0 0.3 fusion.71
  22.3 0.3 fusion.72
  22.7 0.3 fusion.73
  23.0 0.3 fusion.74
  23.3 0.5 fusion.49
  23.8 0.5 fusion.62
  25.4 0.3 fusion.36
  25.7 0.3 fusion.31
  26.0 0.3 fusion.32
  26.3 1.0 fusion.83
  27.3 0.3 fusion.33
  27.8 1.0 fusion.34
  29.5 0.9 fusion.40
  30.6 0.9 fusion.39
  31.8 0.9 fusion.38
  33.0 1.8 copy.215
  34.8 0.8 copy.216
  35.6 1.9 pad_maximum_fusion
  37.5 1.3 collective-permute-start.4
  38.8 1.8 copy.217
  40.6 0.8 copy.218
  41.4 1.9 pad_maximum_fusion.1
  43.4 1.3 collective-permute-start.5
  44.7 0.9 copy.219
  45.5 0.8 copy.220
  46.5 1.8 pad_maximum_fusion.2
  48.3 1.3 collective-permute-start.6
  50.1 0.8 pad_maximum_fusion.3
  51.0 1.3 collective-permute-start.7
  53.0 0.7 copy-done.4
  54.0 0.9 copy.212.grad_query_ref
  54.9 8.1 %collective-permute-done.5 = f32[128,1024]{1,0:T(8,128)} collective-permute-done((f32[128,1024]{1,0:T(8,128)}, f32[128,1024]{1,0:T(8,128)}, u32[]{:S(2)}, u32[]{:S(2)}) %collective-permute-start.5) | collective-permute-done | bytes 524320 | tf_op jit(solution)/shard_map/ppermute | solution.py:20
  63.0 13.2 %collective-permute-done.6 = f32[128,1024]{1,0:T(8,128)} collective-permute-done((f32[128,1024]{1,0:T(8,128)}, f32[128,1024]{1,0:T(8,128)}, u32[]{:S(2)}, u32[]{:S(2)}) %collective-permute-start.6) | collective-permute-done | bytes 524320 | tf_op jit(solution)/shard_map/ppermute | solution.py:20
  76.2 18.6 %collective-permute-done.7 = f32[128,1024]{1,0:T(8,128)S(1)} collective-permute-done((f32[128,1024]{1,0:T(8,128)}, f32[128,1024]{1,0:T(8,128)S(1)}, u32[]{:S(2)}, u32[]{:S(2)}) %collective-permute-start.7) | collective-permute-done | bytes 524320 | tf_op jit(solution)/shard_map/ppermute | solution.py:20
  94.8 2.2 fusion.45.grad_kv_ref
  97.0 125.2 %shard_map.82 = bf16[4,168,512]{2,1,0:T(8,128)(2,1)} custom-call(bf16[128,1024]{1,0:T(8,128)(2,1)} %copy.212.grad_query_ref, bf16[128,1024]{1,0:T(8,128)(2,1)} %fusion.45.grad_kv_ref, bf16[336,1024]{1,0:T(8,128)(2,1)} %bitcast.344, bf16[336,512]{1,0:T(8,128)(2,1)} %bitcast.358, bf16[336,512]{1,0:T(8,128)(2,1)} %bitcast.359), custom_call_target="tpu_custom_call" | custom-call | tf_op jit(solution)/shard_map/pallas_call | solution.py:274
  222.2 1.5 copy.132
  223.6 1.4 broadcast_in_dim_reshape.3
  (58 shorter events, 5.3 us)
Async XLA Ops:
  0.0 1.1 copy-start.6
  1.2 20.7 %collective-permute-start.3 = (bf16[128,1024]{0,1:T(8,128)(2,1)S(1)}, bf16[128,1024]{0,1:T(8,128)(2,1)S(1)}, u32[]{:S(2)}, u32[]{:S(2)}) collective-permute-start(bf16[128,1024]{0,1:T(8,128)(2,1)S(1)} %pad_maximum_fusion.4), channel_id=1, source_target_pairs={{0,2},{2,4},{4,6},{6,8},{8,10},{10,12},{12,14},{14,16},{16,18},{18... | collective-permute-start | bytes 786440 | tf_op jit(solution)/shard_map/ppermute | solution.py:20
  5.3 17.0 %collective-permute-start.2 = (bf16[128,1024]{0,1:T(8,128)(2,1)S(1)}, bf16[128,1024]{0,1:T(8,128)(2,1)S(1)}, u32[]{:S(2)}, u32[]{:S(2)}) collective-permute-start(bf16[128,1024]{0,1:T(8,128)(2,1)S(1)} %pad_maximum_fusion.4), channel_id=1, source_target_pairs={{0,4},{2,6},{4,8},{6,10},{8,12},{10,14},{12,16},{14,18},{16,20},{1... | collective-permute-start | bytes 786440 | tf_op jit(solution)/shard_map/ppermute | solution.py:20
  9.8 12.8 %collective-permute-start = (bf16[128,1024]{0,1:T(8,128)(2,1)S(1)}, bf16[128,1024]{0,1:T(8,128)(2,1)S(1)}, u32[]{:S(2)}, u32[]{:S(2)}) collective-permute-start(bf16[128,1024]{0,1:T(8,128)(2,1)S(1)} %pad_maximum_fusion.4), channel_id=1, source_target_pairs={{0,8},{2,10},{4,12},{6,14},{8,16},{10,18},{12,20},{14,22},{16,24},... | collective-permute-start | bytes 786440 | tf_op jit(solution)/shard_map/ppermute | solution.py:20
  13.4 9.6 %collective-permute-start.1 = (bf16[128,1024]{0,1:T(8,128)(2,1)S(1)}, bf16[128,1024]{0,1:T(8,128)(2,1)S(1)}, u32[]{:S(2)}, u32[]{:S(2)}) collective-permute-start(bf16[128,1024]{0,1:T(8,128)(2,1)S(1)} %pad_maximum_fusion.4), channel_id=1, source_target_pairs={{0,6},{2,8},{4,10},{6,12},{8,14},{10,16},{12,18},{14,20},{16,22},{... | collective-permute-start | bytes 786440 | tf_op jit(solution)/shard_map/ppermute | solution.py:20
  17.7 0.7 copy-start.9
  18.5 0.9 copy-start.5
  19.4 0.9 copy-start.7
  20.5 1.0 copy-start.8
  37.5 17.4 %collective-permute-start.4 = (f32[128,1024]{1,0:T(8,128)}, f32[128,1024]{1,0:T(8,128)}, u32[]{:S(2)}, u32[]{:S(2)}) collective-permute-start(f32[128,1024]{1,0:T(8,128)} %pad_maximum_fusion), channel_id=1, source_target_pairs={{2,0},{4,2},{6,4},{8,6},{10,8},{12,10},{14,12},{16,14},{18,16},{20... | collective-permute-start | bytes 1572872 | tf_op jit(solution)/shard_map/ppermute | solution.py:20
  38.8 1.8 copy-start
  41.4 3.2 %copy-start.1 = (f32[4,128,128]{1,2,0:T(8,128)S(1)}, f32[4,128,128]{1,2,0:T(8,128)}, u32[]{:S(2)}) copy-start(f32[4,128,128]{1,2,0:T(8,128)} %fusion.40) | copy-start | bytes 786436
  43.4 19.6 %collective-permute-start.5 = (f32[128,1024]{1,0:T(8,128)}, f32[128,1024]{1,0:T(8,128)}, u32[]{:S(2)}, u32[]{:S(2)}) collective-permute-start(f32[128,1024]{1,0:T(8,128)} %pad_maximum_fusion.1), channel_id=1, source_target_pairs={{4,0},{6,2},{8,4},{10,6},{12,8},{14,10},{16,12},{18,14},{20,16},{2... | collective-permute-start | bytes 1572872 | tf_op jit(solution)/shard_map/ppermute | solution.py:20
  45.5 0.9 copy-start.2
  46.5 3.1 %copy-start.3 = (bf16[4,2,128,128]{2,3,1,0:T(8,128)(2,1)S(1)}, bf16[4,2,128,128]{2,3,1,0:T(8,128)(2,1)}, u32[]{:S(2)}) copy-start(bf16[4,2,128,128]{2,3,1,0:T(8,128)(2,1)} %fusion.34) | copy-start | bytes 786436
  48.3 27.8 %collective-permute-start.6 = (f32[128,1024]{1,0:T(8,128)}, f32[128,1024]{1,0:T(8,128)}, u32[]{:S(2)}, u32[]{:S(2)}) collective-permute-start(f32[128,1024]{1,0:T(8,128)} %pad_maximum_fusion.2), channel_id=1, source_target_pairs={{6,0},{8,2},{10,4},{12,6},{14,8},{16,10},{18,12},{20,14},{22,16},{... | collective-permute-start | bytes 1572872 | tf_op jit(solution)/shard_map/ppermute | solution.py:20
  51.0 43.8 %collective-permute-start.7 = (f32[128,1024]{1,0:T(8,128)}, f32[128,1024]{1,0:T(8,128)S(1)}, u32[]{:S(2)}, u32[]{:S(2)}) collective-permute-start(f32[128,1024]{1,0:T(8,128)} %pad_maximum_fusion.3), channel_id=1, source_target_pairs={{8,0},{10,2},{12,4},{14,6},{16,8},{18,10},{20,12},{22,14},{24,16},... | collective-permute-start | bytes 1572872 | tf_op jit(solution)/shard_map/ppermute | solution.py:20
  52.8 1.0 copy-start.4

commit v2 on v1

--- a/solution.py
+++ b/solution.py
@@ -1,4 +1,3 @@
-from functools import reduce
 import math
 
 import jax
@@ -12,15 +11,312 @@
 WINDOW = 512
 RING = 4
 MESH = pl.DeviceIdType.MESH
-
-
-def from_behind(shard, axis, by):
-    size = lax.axis_size(axis)
-    pairs = [(i, i + by) for i in range(size) if 0 <= i + by < size]
-    return lax.ppermute(shard, axis, pairs)
-
-
 NT = (((1,), (1,)), ((), ()))
+TN = (((0,), (0,)), ((), ()))
+
+
+def attention_kernel(
+    docs_ref,
+    query_ref,
+    key_ref,
+    value_ref,
+    grad_ref,
+    query_out,
+    kv_out,
+    keys,
+    values,
+    bias,
+    sums,
+    returned,
+    returns_in,
+    behind,
+    behind_in,
+    own_sem,
+    halo_send,
+    halo_recv,
+    back_send,
+    back_recv,
+    line_send,
+    line_recv,
+):
+    seq_place = lax.axis_index("seq")
+    run = seq_place // RING
+    turn = lax.rem(seq_place, RING)
+    rows = query_ref.shape[0]
+    heads = key_ref.shape[1] // HEAD_WIDTH
+    scaling = 1.0 / math.sqrt(HEAD_WIDTH)
+    near = range(1, RING)
+
+    barrier = pltpu.get_barrier_semaphore()
+    for step in near:
+        pl.semaphore_signal(
+            barrier,
+            inc=1,
+            device_id={"seq": run * RING + lax.rem(turn + step, RING)},
+            device_id_type=MESH,
+        )
+
+    @pl.when(run < RING - 1)
+    def _():
+        pl.semaphore_signal(barrier, inc=1, device_id={"seq": seq_place + RING}, device_id_type=MESH)
+
+    @pl.when(run > 0)
+    def _():
+        pl.semaphore_signal(barrier, inc=1, device_id={"seq": seq_place - RING}, device_id_type=MESH)
+
+    in_line = (run > 0).astype(jnp.int32) + (run < RING - 1).astype(jnp.int32)
+    pl.semaphore_wait(barrier, RING - 1 + in_line)
+
+    sources = (key_ref, value_ref)
+    buffers = (keys, values)
+
+    def slot(step):
+        return pl.ds((RING - step) * rows, rows)
+
+    def head_of(ref, head):
+        return ref.at[:, pl.ds(head * HEAD_WIDTH, HEAD_WIDTH)]
+
+    def own_copy(kind, head):
+        return pltpu.make_async_copy(
+            head_of(sources[kind], head), buffers[kind].at[head, slot(0)], own_sem.at[kind, head]
+        )
+
+    def halo_copy(kind, head, step, relayed):
+        if step == RING:
+            to = seq_place + RING
+        else:
+            to = run * RING + lax.rem(turn + step, RING)
+        source = buffers[kind].at[head, slot(RING)] if relayed else head_of(sources[kind], head)
+        return pltpu.make_async_remote_copy(
+            src_ref=source,
+            dst_ref=buffers[kind].at[head, slot(step)],
+            send_sem=halo_send.at[kind, step - 1, head],
+            recv_sem=halo_recv.at[kind, step - 1, head],
+            device_id={"seq": to},
+            device_id_type=MESH,
+        )
+
+    def send_own(head):
+        @pl.when(run < RING - 1)
+        def _():
+            for kind in (0, 1):
+                halo_copy(kind, head, RING, False).start()
+
+        for step in near:
+
+            @pl.when(turn + step < RING)
+            def _():
+                for kind in (0, 1):
+                    halo_copy(kind, head, step, False).start()
+
+    def send_relayed(head):
+        @pl.when(run > 0)
+        def _():
+            for kind in (0, 1):
+                halo_copy(kind, head, RING, False).wait_recv()
+            for step in near:
+
+                @pl.when(turn + step >= RING)
+                def _():
+                    for kind in (0, 1):
+                        halo_copy(kind, head, step, True).start()
+
+    def wait_halo(head):
+        for kind in (0, 1):
+            own_copy(kind, head).wait()
+        for step in near:
+
+            @pl.when(seq_place >= step)
+            def _():
+                for kind in (0, 1):
+                    halo_copy(kind, head, step, False).wait_recv()
+
+    def back_copy(head, step):
+        return pltpu.make_async_remote_copy(
+            src_ref=returned.at[head, step - 1],
+            dst_ref=returns_in.at[head, step - 1],
+            send_sem=back_send.at[head, step - 1],
+            recv_sem=back_recv.at[head, step - 1],
+            device_id={"seq": run * RING + lax.rem(turn + RING - step, RING)},
+            device_id_type=MESH,
+        )
+
+    def line_copy(head):
+        return pltpu.make_async_remote_copy(
+            src_ref=behind.at[head],
+            dst_ref=behind_in.at[head],
+            send_sem=line_send.at[head],
+            recv_sem=line_recv.at[head],
+            device_id={"seq": seq_place - RING},
+            device_id_type=MESH,
+        )
+
+    def both(ref, head):
+        block = ref[:, 2 * head * HEAD_WIDTH : 2 * (head + 1) * HEAD_WIDTH]
+        return jnp.concatenate([block[:, :HEAD_WIDTH], block[:, HEAD_WIDTH:]], axis=0)
+
+    def attend(head):
+        query = both(query_ref, head)
+        grad = both(grad_ref, head)
+        key = keys[head]
+        value = values[head]
+        scores = lax.dot_general(query, key, NT, preferred_element_type=jnp.float32)
+        mask = jnp.concatenate([bias[...], bias[...]], axis=0)
+        scores = scores * scaling + mask
+        raised = jnp.exp(scores - jnp.max(scores, axis=1, keepdims=True))
+        weights = raised * (1.0 / jnp.sum(raised, axis=1, keepdims=True))
+        weights_half = weights.astype(jnp.bfloat16)
+        attended = jnp.dot(weights_half, value, preferred_element_type=jnp.float32)
+        delta = jnp.sum(grad.astype(jnp.float32) * attended, axis=1, keepdims=True)
+        grad_weights = lax.dot_general(grad, value, NT, preferred_element_type=jnp.float32)
+        grad_scores = (weights * (grad_weights - delta)).astype(jnp.bfloat16)
+        grad_query = jnp.dot(grad_scores, key, preferred_element_type=jnp.float32) * scaling
+        grad_query = grad_query.astype(jnp.bfloat16)
+        first = 2 * head * HEAD_WIDTH
+        query_out[:, first : first + HEAD_WIDTH] = grad_query[:rows]
+        query_out[:, first + HEAD_WIDTH : first + 2 * HEAD_WIDTH] = grad_query[rows:]
+        grads = (
+            lax.dot_general(grad_scores, query, TN, preferred_element_type=jnp.float32) * scaling,
+            lax.dot_general(weights_half, grad, TN, preferred_element_type=jnp.float32),
+        )
+        for kind in (0, 1):
+            sums[head, 0, kind] = grads[kind][RING * rows :]
+            sums[head, 1, kind] = grads[kind][:rows]
+            for step in near:
+                first = (RING - step) * rows
+                returned[head, step - 1, kind] = grads[kind][first : first + rows].astype(jnp.bfloat16)
+        for step in near:
+
+            @pl.when(seq_place >= step)
+            def _():
+                back_copy(head, step).start()
+
+    def collect_behind(head):
+        @pl.when(run > 0)
+        def _():
+            for step in near:
+
+                @pl.when(turn + step >= RING)
+                def _():
+                    back_copy(head, step).wait_recv()
+                    sums[head, 1] += returns_in[head, step - 1].astype(jnp.float32)
+
+            behind[head] = sums[head, 1].astype(jnp.bfloat16)
+            line_copy(head).start()
+
+    def collect_own(head):
+        for step in near:
+
+            @pl.when(turn + step < RING)
+            def _():
+                back_copy(head, step).wait_recv()
+                sums[head, 0] += returns_in[head, step - 1].astype(jnp.float32)
+
+        @pl.when(run < RING - 1)
+        def _():
+            line_copy(head).wait_recv()
+            sums[head, 0] += behind_in[head].astype(jnp.float32)
+
+        for kind in (0, 1):
+            first = (kind * heads + head) * HEAD_WIDTH
+            kv_out[:, first : first + HEAD_WIDTH] = sums[head, 0, kind].astype(jnp.bfloat16)
+
+    for head in range(heads):
+        for kind in (0, 1):
+            own_copy(kind, head).start()
+        send_own(head)
+        if head >= 1:
+            send_relayed(head - 1)
+    send_relayed(heads - 1)
+
+    for step in range(1, RING + 1):
+
+        @pl.when(seq_place < step)
+        def _():
+            for buffer in buffers:
+                for head in range(heads):
+                    buffer[head, slot(step)] = jnp.zeros((rows, HEAD_WIDTH), jnp.bfloat16)
+
+    first_row = pl.multiple_of(seq_place * rows, rows)
+    here = docs_ref[:, pl.ds(first_row, rows)].astype(jnp.float32)
+    query_docs = jnp.transpose(jnp.broadcast_to(here, (rows, rows)))
+    query_row = lax.broadcasted_iota(jnp.int32, (rows, rows), 0)
+    key_row = lax.broadcasted_iota(jnp.int32, (rows, rows), 1)
+    for step in range(RING + 1):
+        start = pl.multiple_of(jnp.maximum(seq_place - step, 0) * rows, rows)
+        there = docs_ref[:, pl.ds(start, rows)].astype(jnp.float32)
+        offset = query_row - key_row + step * rows
+        allowed = (query_docs == there) & (offset >= 0) & (offset < WINDOW)
+        allowed = allowed & (jnp.full((rows, rows), seq_place, jnp.int32) >= step)
+        bias[:, (RING - step) * rows : (RING - step + 1) * rows] = jnp.where(
+            allowed, 0.0, -jnp.inf
+        )
+
+    for head in range(heads):
+        wait_halo(head)
+        attend(head)
+        if head >= 1:
+            collect_behind(head - 1)
+    collect_behind(heads - 1)
+    for head in range(heads):
+        collect_own(head)
+
+    for head in range(heads):
+        for kind in (0, 1):
+            for step in near:
+
+                @pl.when((turn + step < RING) | (run > 0))
+                def _():
+                    halo_copy(kind, head, step, False).wait_send()
+
+            @pl.when(run < RING - 1)
+            def _():
+                halo_copy(kind, head, RING, False).wait_send()
+
+        for step in near:
+
+            @pl.when(seq_place >= step)
+            def _():
+                back_copy(head, step).wait_send()
+
+        @pl.when(run > 0)
+        def _():
+            line_copy(head).wait_send()
+
+
+def attention_grads(docs, query, key, value, grad):
+    rows = query.shape[0]
+    heads = key.shape[1] // HEAD_WIDTH
+    dma = pltpu.SemaphoreType.DMA
+    whole = pl.BlockSpec(memory_space=pltpu.VMEM)
+    tile = (rows, HEAD_WIDTH)
+    return pl.pallas_call(
+        attention_kernel,
+        out_shape=(
+            jax.ShapeDtypeStruct(query.shape, jnp.bfloat16),
+            jax.ShapeDtypeStruct((rows, 2 * key.shape[1]), jnp.bfloat16),
+        ),
+        in_specs=[whole] * 5,
+        out_specs=(whole, whole),
+        scratch_shapes=[
+            pltpu.VMEM((heads, (RING + 1) * rows, HEAD_WIDTH), jnp.bfloat16),
+            pltpu.VMEM((heads, (RING + 1) * rows, HEAD_WIDTH), jnp.bfloat16),
+            pltpu.VMEM((rows, (RING + 1) * rows), jnp.float32),
+            pltpu.VMEM((heads, 2, 2) + tile, jnp.float32),
+            pltpu.VMEM((heads, RING - 1, 2) + tile, jnp.bfloat16),
+            pltpu.VMEM((heads, RING - 1, 2) + tile, jnp.bfloat16),
+            pltpu.VMEM((heads, 2) + tile, jnp.bfloat16),
+            pltpu.VMEM((heads, 2) + tile, jnp.bfloat16),
+            dma((2, heads)),
+            dma((2, RING, heads)),
+            dma((2, RING, heads)),
+            dma((heads, RING - 1)),
+            dma((heads, RING - 1)),
+            dma((heads,)),
+            dma((heads,)),
+        ],
+        compiler_params=pltpu.CompilerParams(collective_id=1, has_side_effects=True),
+    )(docs, query, key, value, grad)
 
 
 def spread_kernel(
@@ -301,151 +597,10 @@
     value_weight,
     doc_ids,
 ):
-    query_here = query_rows[0]
-    key_here = key_row_matrix[0]
-    value_here = value_row_matrix[0]
-    grad_here = out_grad[0]
-    documents = doc_ids[0]
-    row_count = query_here.shape[0]
-    kv_cols = key_here.shape[1]
-    kv_heads = kv_cols // HEAD_WIDTH
-    group_width = query_here.shape[1] // kv_cols
-    scaling = 1.0 / math.sqrt(HEAD_WIDTH)
-    seq_count = lax.axis_size("seq")
-    seq_place = lax.axis_index("seq")
-    reach_now = min((WINDOW - 1) // row_count + 1, seq_count - 1)
-    kv_local = jnp.concatenate([key_here, value_here], axis=1)
-    rim_blocks = [from_behind(kv_local, "seq", distance) for distance in range(reach_now, 0, -1)]
-    kv_blocks = rim_blocks + [kv_local]
-    block_total = len(kv_blocks)
-    span_rows = block_total * row_count
-    first_row = seq_place * row_count
-    padded_docs = jnp.concatenate([jnp.full((reach_now * row_count,), -1, jnp.int32), documents])
-    key_docs = lax.dynamic_slice_in_dim(padded_docs, first_row, span_rows, 0)
-    query_docs = lax.dynamic_slice_in_dim(documents, first_row, row_count, 0)
-    query_pos = first_row + jnp.arange(row_count, dtype=jnp.int32)
-    key_pos = first_row - reach_now * row_count + jnp.arange(span_rows, dtype=jnp.int32)
-    offset = query_pos[:, None] - key_pos[None, :]
-    allowed = (query_docs[:, None] == key_docs[None, :]) & (offset >= 0) & (offset < WINDOW)
-    query_split = query_here.reshape(row_count, kv_heads, group_width, HEAD_WIDTH)
-    grad_split = grad_here.reshape(row_count, kv_heads, group_width, HEAD_WIDTH)
-    block_masks = [
-        allowed[:, block_index * row_count : (block_index + 1) * row_count]
-        for block_index in range(block_total)
-    ]
-    block_keys = [
-        kv_block[:, :kv_cols].reshape(row_count, kv_heads, HEAD_WIDTH) for kv_block in kv_blocks
-    ]
-    block_values = [
-        kv_block[:, kv_cols:].reshape(row_count, kv_heads, HEAD_WIDTH) for kv_block in kv_blocks
-    ]
-
-    def score_pair(key_block, mask_now):
-
-        def make_fn():
-            product = (
-                jnp.einsum(
-                    "igrd,jgd->grij", query_split, key_block, preferred_element_type=jnp.float32
-                )
-                * scaling
-            )
-            return jnp.where(mask_now[None, None], product, -jnp.inf)
-
-        def empty_fn():
-            return jnp.full((kv_heads, group_width, row_count, row_count), -jnp.inf, jnp.float32)
-
-        return (make_fn, empty_fn)
-
-    scores = []
-    for block_index in range(block_total):
-        make_fn, empty_fn = score_pair(block_keys[block_index], block_masks[block_index])
-        scores.append(make_fn())
-    row_max = reduce(
-        jnp.maximum, [jnp.max(score_now, axis=-1, keepdims=True) for score_now in scores]
+    grad_query, grad_kv = attention_grads(
+        doc_ids, query_rows[0], key_row_matrix[0], value_row_matrix[0], out_grad[0]
     )
-    raised = [jnp.exp(score_now - row_max) for score_now in scores]
-    row_total = reduce(
-        jnp.add, [jnp.sum(raised_now, axis=-1, keepdims=True) for raised_now in raised]
-    )
-    weights_full = [raised_now / row_total for raised_now in raised]
-    weights_half = [weight_now.astype(jnp.bfloat16) for weight_now in weights_full]
-
-    def value_pair(weight_half, value_block):
-
-        def make_fn():
-            return jnp.einsum(
-                "grij,jgd->igrd", weight_half, value_block, preferred_element_type=jnp.float32
-            )
-
-        def empty_fn():
-            return jnp.zeros((row_count, kv_heads, group_width, HEAD_WIDTH), jnp.float32)
-
-        return (make_fn, empty_fn)
-
-    attended_terms = []
-    for block_index in range(block_total):
-        make_fn, empty_fn = value_pair(weights_half[block_index], block_values[block_index])
-        attended_terms.append(make_fn())
-    attended = reduce(jnp.add, attended_terms)
-    delta_row = jnp.transpose(
-        jnp.sum(grad_split.astype(jnp.float32) * attended, axis=-1), (1, 2, 0)
-    )
-
-    def grad_pair(weight_full, weight_half, key_block, value_block):
-
-        def make_fn():
-            grad_weights = jnp.einsum(
-                "igrd,jgd->grij", grad_split, value_block, preferred_element_type=jnp.float32
-            )
-            grad_scores = (weight_full * (grad_weights - delta_row[..., None])).astype(jnp.bfloat16)
-            query_term = jnp.einsum(
-                "grij,jgd->igrd", grad_scores, key_block, preferred_element_type=jnp.float32
-            )
-            key_term = (
-                jnp.einsum(
-                    "grij,igrd->jgd", grad_scores, query_split, preferred_element_type=jnp.float32
-                )
-                * scaling
-            )
-            value_term = jnp.einsum(
-                "grij,igrd->jgd", weight_half, grad_split, preferred_element_type=jnp.float32
-            )
-            kv_term = jnp.concatenate(
-                [key_term.reshape(row_count, kv_cols), value_term.reshape(row_count, kv_cols)],
-                axis=1,
-            )
-            return (query_term, kv_term)
-
-        def empty_fn():
-            return (
-                jnp.zeros((row_count, kv_heads, group_width, HEAD_WIDTH), jnp.float32),
-                jnp.zeros((row_count, 2 * kv_cols), jnp.float32),
-            )
-
-        return (make_fn, empty_fn)
-
-    query_terms = []
-    kv_terms = []
-    for block_index in range(block_total):
-        make_fn, empty_fn = grad_pair(
-            weights_full[block_index],
-            weights_half[block_index],
-            block_keys[block_index],
-            block_values[block_index],
-        )
-        query_term, kv_term = make_fn()
-        query_terms.append(query_term)
-        kv_terms.append(kv_term)
-    query_grad = (
-        (reduce(jnp.add, query_terms) * scaling)
-        .astype(jnp.bfloat16)
-        .reshape(row_count, kv_heads * group_width * HEAD_WIDTH)
-    )
-    kv_total = kv_terms[-1]
-    for distance in range(1, reach_now + 1):
-        kv_total = kv_total + from_behind(kv_terms[reach_now - distance], "seq", -distance)
-    kv_half = kv_total.astype(jnp.bfloat16)
-    upstream = spread_and_project(query_grad, kv_half, w_query[0], key_weight[0], value_weight[0])
+    upstream = spread_and_project(grad_query, grad_kv, w_query[0], key_weight[0], value_weight[0])
     return upstream[None]
 
 

time: 226 us -> 167 us (0.74)
  waiting for transfers between devices: 39.9 us -> 0 us
  Pallas kernels: 125 us -> 163 us
  starting transfers between devices: 21.6 us -> 0 us
  local copies, waits for them, and re-layouts: 16.8 us -> 2.81 us
  matrix products: 10.9 us -> 0 us
  other arithmetic: 10 us -> 0 us
    ppermute x8 -> x0, waiting for transfers between devices: 39.9 us -> none  [from_behind(): return lax.ppermute(shard, axis, pairs)]
    pallas_call x0 -> x1, Pallas kernels: none -> 27.9 us  [attention_grads(): pl.pallas_call(attention_kernel, out_shape=(jax.ShapeDtypeStruct(query.sh...]
    ppermute x8 -> x0, starting transfers between devices: 21.6 us -> none  [from_behind(): return lax.ppermute(shard, axis, pairs)]
    dot_general x30 -> x0, matrix products: 10.9 us -> none  [the longest x5 3.29 us: make_fn(): jnp.einsum('grij,igrd->jgd', grad_scores, query_split, preferred_element_...]
    pallas_call x1, Pallas kernels: 125 us -> 135 us  [spread_and_project(): pl.pallas_call(spread_kernel, out_shape=jax.ShapeDtypeStruct((RING, width...]
    reshape x11 -> x0, local copies, waits for them, and re-layouts: 8.38 us -> none  [the longest x5 4.73 us: make_fn(): key_term.reshape(row_count, kv_cols)]
    concatenate x5 -> x0, other arithmetic: 6.49 us -> none  [the longest x4 6.47 us: make_fn(): jnp.concatenate([key_term.reshape(row_count, kv_cols), value_term.reshape...]
    unnamed x23 -> x0, local copies, waits for them, and re-layouts: 5.2 us -> none
  transfers between devices with their start and end apart: 8 -> 0, of which waited for: 3 -> 0; matrix products, arithmetic and copies ran while one was open for 6% -> 0% of each run, Pallas kernels for 0% -> 0%
where the time goes in v2:
time: 167 us; the launch traced here: 166 us
  Pallas kernels  163 us (98%)
  local copies, waits for them, and re-layouts  2.81 us (2%)
    pallas_call x1, Pallas kernels, spread_and_project(): pl.pallas_call(spread_kernel, out_shape=jax.ShapeDtypeStruct((RING, width...  135 us
    pallas_call x1, Pallas kernels, attention_grads(): pl.pallas_call(attention_kernel, out_shape=(jax.ShapeDtypeStruct(query.sh...  27.9 us

profile of v2, /device:TPU:1, one launch (start us, length us, event | category | flops | bytes accessed | tf_op | source)
XLA Modules:
  0.0 166.0 jit_solution(12327871110049493376)
XLA Ops:
  0.0 27.9 %shard_map.82 = (bf16[128,1024]{1,0:T(8,128)(2,1)}, bf16[128,1024]{1,0:T(8,128)(2,1)}) custom-call(s32[1,2048]{1,0:T(1,128)} %docs_ref.1, bf16[128,1024]{1,0:T(8,128)(2,1)} %bitcast.14, bf16[128,512]{1,0:T(8,128)(2,1)} %bitcast.16, bf16[128,512]{1,0:T(8,128)(2,1)} %bitcast.17, bf16[128,1024]{1,0:T(8,128)(2,1)} %bitcast.15), custom_call_target="tpu_custom_call" | custom-call | tf_op jit(solution)/shard_map/pallas_call | solution.py:293
  27.9 135.3 %shard_map.83 = bf16[4,168,512]{2,1,0:T(8,128)(2,1)} custom-call(bf16[128,1024]{1,0:T(8,128)(2,1)} %get-tuple-element.7.grad_query_ref, bf16[128,1024]{1,0:T(8,128)(2,1)} %get-tuple-element.8.grad_kv_ref, bf16[336,1024]{1,0:T(8,128)(2,1)} %bitcast.11, bf16[336,512]{1,0:T(8,128)(2,1)} %bitcast.12, bf16[336,512]{1,0:T(8,128)(2,1)} %bitcast.13), custom_call_target="tpu_custom_call" | custom-call | tf_op jit(solution)/shard_map/pallas_call | solution.py:570
  163.2 1.5 copy.9
  164.7 1.4 broadcast_in_dim_reshape.3

commit v3 on v2

v3 whole, which is shorter than its diff:
```python
import math

import jax
import jax.numpy as jnp
from jax import lax
from jax.experimental import pallas as pl
from jax.experimental.pallas import tpu as pltpu
from jax.sharding import PartitionSpec as P

HEAD_WIDTH = 128
WINDOW = 512
RING = 4
LEG = 6
MESH = pl.DeviceIdType.MESH
NT = (((1,), (1,)), ((), ()))
TN = (((0,), (0,)), ((), ()))
PIECES = 4
PIECE_HEADS = 4
EARLY_WEIGHTS = 2


def signal(semaphore, device):
    pl.semaphore_signal(semaphore, inc=1, device_id=device, device_id_type=MESH)


def cascade_kernel(
    docs_ref,
    query_ref,
    key_ref,
    value_ref,
    grad_ref,
    w_query_ref,
    key_weight_ref,
    value_weight_ref,
    out_ref,
    keys,
    values,
    bias,
    sums,
    returned,
    returns_in,
    behind,
    behind_in,
    held,
    weights_in,
    part,
    part_in,
    ready,
    relayed,
    landed,
    own_sem,
    halo_send,
    halo_recv,
    back_send,
    back_recv,
    line_send,
    line_recv,
    weight_send,
    weight_recv,
    across_send,
    across_recv,
    right_send,
    right_recv,
    left_send,
    left_recv,
    far_right_send,
    far_right_recv,
    far_left_send,
    far_left_recv,
    core_send,
    core_recv,
    section_send,
    section_recv,
    relay_recv,
    forward_send,
):
    seq_place = lax.axis_index("seq")
    core = lax.axis_index("mp")
    section = lax.axis_index("section")
    section_count = lax.axis_size("section")
    run = seq_place // RING
    turn = lax.rem(seq_place, RING)
    column = section // RING
    block = lax.rem(section, RING)
    rows = query_ref.shape[0]
    half = rows // 2
    heads = key_ref.shape[1] // HEAD_WIDTH
    width = w_query_ref.shape[0] // 2
    scaling = 1.0 / math.sqrt(HEAD_WIDTH)
    near = range(1, RING)

    right = run * RING + lax.rem(turn + 1, RING)
    left = run * RING + lax.rem(turn + RING - 1, RING)
    paired_run = run + 1 - 2 * lax.rem(run, 2)
    paired = paired_run * RING + turn
    opposite_run = lax.rem(run + 2, RING)
    opposite = opposite_run * RING + turn
    back_section = lax.rem(section + section_count - 1, section_count)
    next_section = lax.rem(section + 1, section_count)

    depth = RING * RING
    along = block * RING + run
    ahead = lax.rem(along + LEG, depth)
    before = lax.rem(along + depth - LEG, depth)

    def at(col, place):
        return {"section": col * RING + place // RING, "seq": lax.rem(place, RING) * RING + turn}

    turned = block == 0
    from_turned = before < RING
    first_column = lax.rem(column + RING - turned.astype(jnp.int32), RING)
    source_column = lax.rem(column + from_turned.astype(jnp.int32), RING)

    barrier = pltpu.get_barrier_semaphore()
    for step in near:
        signal(barrier, {"seq": run * RING + lax.rem(turn + step, RING)})
    signal(barrier, {"seq": opposite})
    signal(barrier, {"mp": 1 - core})
    for place in (seq_place, paired):
        signal(barrier, {"section": back_section, "seq": place})
        signal(barrier, {"section": next_section, "seq": place})
    signal(barrier, at(column, ahead))
    signal(barrier, at(column, before))

    @pl.when(turned)
    def _():
        signal(barrier, at(first_column, ahead))

    @pl.when(from_turned)
    def _():
        signal(barrier, at(source_column, before))

    @pl.when(run < RING - 1)
    def _():
        signal(barrier, {"seq": seq_place + RING})

    @pl.when(run > 0)
    def _():
        signal(barrier, {"seq": seq_place - RING})

    peers = RING - 1 + 1 + 1 + 4 + 2
    peers = peers + turned.astype(jnp.int32) + from_turned.astype(jnp.int32)
    peers = peers + (run > 0).astype(jnp.int32) + (run < RING - 1).astype(jnp.int32)
    pl.semaphore_wait(barrier, peers)

    sources = (key_ref, value_ref)
    buffers = (keys, values)

    def slot(step):
        return pl.ds((RING - step) * rows, rows)

    def head_of(ref, head):
        return ref.at[:, pl.ds(head * HEAD_WIDTH, HEAD_WIDTH)]

    def own_copy(kind, head):
        return pltpu.make_async_copy(
            head_of(sources[kind], head), buffers[kind].at[head, slot(0)], own_sem.at[kind, head]
        )

    def halo_copy(kind, head, step, relayed):
        if step == RING:
            to = seq_place + RING
        else:
            to = run * RING + lax.rem(turn + step, RING)
        source = buffers[kind].at[head, slot(RING)] if relayed else head_of(sources[kind], head)
        return pltpu.make_async_remote_copy(
            src_ref=source,
            dst_ref=buffers[kind].at[head, slot(step)],
            send_sem=halo_send.at[kind, step - 1, head],
            recv_sem=halo_recv.at[kind, step - 1, head],
            device_id={"seq": to},
            device_id_type=MESH,
        )

    def send_own(head):
        @pl.when(run < RING - 1)
        def _():
            for kind in (0, 1):
                halo_copy(kind, head, RING, False).start()

        for step in near:

            @pl.when(turn + step < RING)
            def _():
                for kind in (0, 1):
                    halo_copy(kind, head, step, False).start()

    def send_relayed(head):
        @pl.when(run > 0)
        def _():
            for kind in (0, 1):
                halo_copy(kind, head, RING, False).wait_recv()
            for step in near:

                @pl.when(turn + step >= RING)
                def _():
                    for kind in (0, 1):
                        halo_copy(kind, head, step, True).start()

    def wait_halo(head):
        for kind in (0, 1):
            own_copy(kind, head).wait()
        for step in near:

            @pl.when(seq_place >= step)
            def _():
                for kind in (0, 1):
                    halo_copy(kind, head, step, False).wait_recv()

    def back_copy(head, step):
        return pltpu.make_async_remote_copy(
            src_ref=returned.at[head, step - 1],
            dst_ref=returns_in.at[head, step - 1],
            send_sem=back_send.at[head, step - 1],
            recv_sem=back_recv.at[head, step - 1],
            device_id={"seq": run * RING + lax.rem(turn + RING - step, RING)},
            device_id_type=MESH,
        )

    def line_copy(head):
        return pltpu.make_async_remote_copy(
            src_ref=behind.at[head],
            dst_ref=behind_in.at[head],
            send_sem=line_send.at[head],
            recv_sem=line_recv.at[head],
            device_id={"seq": seq_place - RING},
            device_id_type=MESH,
        )

    def both(ref, head):
        block = ref[:, 2 * head * HEAD_WIDTH : 2 * (head + 1) * HEAD_WIDTH]
        return jnp.concatenate([block[:, :HEAD_WIDTH], block[:, HEAD_WIDTH:]], axis=0)

    def attend(head):
        query = both(query_ref, head)
        grad = both(grad_ref, head)
        key = keys[head]
        value = values[head]
        scores = lax.dot_general(query, key, NT, preferred_element_type=jnp.float32)
        mask = jnp.concatenate([bias[...], bias[...]], axis=0)
        scores = scores * scaling + mask
        raised = jnp.exp(scores - jnp.max(scores, axis=1, keepdims=True))
        weights = raised * (1.0 / jnp.sum(raised, axis=1, keepdims=True))
        weights_half = weights.astype(jnp.bfloat16)
        attended = jnp.dot(weights_half, value, preferred_element_type=jnp.float32)
        delta = jnp.sum(grad.astype(jnp.float32) * attended, axis=1, keepdims=True)
        grad_weights = lax.dot_general(grad, value, NT, preferred_element_type=jnp.float32)
        grad_scores = (weights * (grad_weights - delta)).astype(jnp.bfloat16)
        grad_query = jnp.dot(grad_scores, key, preferred_element_type=jnp.float32) * scaling
        grad_query = grad_query.astype(jnp.bfloat16)
        piece, place = divmod(2 * head, PIECE_HEADS)
        first = place * HEAD_WIDTH
        held[piece, 0, turn, :, first : first + HEAD_WIDTH] = grad_query[:rows]
        held[piece, 0, turn, :, first + HEAD_WIDTH : first + 2 * HEAD_WIDTH] = grad_query[rows:]
        grads = (
            lax.dot_general(grad_scores, query, TN, preferred_element_type=jnp.float32) * scaling,
            lax.dot_general(weights_half, grad, TN, preferred_element_type=jnp.float32),
        )
        for kind in (0, 1):
            sums[head, 0, kind] = grads[kind][RING * rows :]
            sums[head, 1, kind] = grads[kind][:rows]
            for step in near:
                first = (RING - step) * rows
                returned[head, step - 1, kind] = grads[kind][first : first + rows].astype(jnp.bfloat16)
        for step in near:

            @pl.when(seq_place >= step)
            def _():
                back_copy(head, step).start()

    def collect_behind(head):
        @pl.when(run > 0)
        def _():
            for step in near:

                @pl.when(turn + step >= RING)
                def _():
                    back_copy(head, step).wait_recv()
                    sums[head, 1] += returns_in[head, step - 1].astype(jnp.float32)

            behind[head] = sums[head, 1].astype(jnp.bfloat16)
            line_copy(head).start()

    def collect_own(head):
        for step in near:

            @pl.when(turn + step < RING)
            def _():
                back_copy(head, step).wait_recv()
                sums[head, 0] += returns_in[head, step - 1].astype(jnp.float32)

        @pl.when(run < RING - 1)
        def _():
            line_copy(head).wait_recv()
            sums[head, 0] += behind_in[head].astype(jnp.float32)

        for kind in (0, 1):
            first = head * HEAD_WIDTH
            held[2 + kind, 0, turn, :, first : first + HEAD_WIDTH] = sums[head, 0, kind].astype(
                jnp.bfloat16
            )


    def weight_piece(piece):
        span = pl.ds(piece * PIECE_HEADS * HEAD_WIDTH, PIECE_HEADS * HEAD_WIDTH)
        return (
            w_query_ref.at[:, span] if piece < 2 else (key_weight_ref, value_weight_ref)[piece - 2]
        )

    def weight_copy(piece):
        return pltpu.make_async_remote_copy(
            src_ref=weight_piece(piece),
            dst_ref=weights_in.at[piece],
            send_sem=weight_send.at[piece],
            recv_sem=weight_recv.at[piece],
            device_id={"seq": paired},
            device_id_type=MESH,
        )

    def across_copy(piece):
        return pltpu.make_async_remote_copy(
            src_ref=held.at[piece, 0, turn],
            dst_ref=held.at[piece, 1, turn],
            send_sem=across_send.at[piece],
            recv_sem=across_recv.at[piece],
            device_id={"seq": opposite},
            device_id_type=MESH,
        )

    def ring_copy(shard, to, send, recv):
        return pltpu.make_async_remote_copy(
            src_ref=shard,
            dst_ref=shard,
            send_sem=send,
            recv_sem=recv,
            device_id={"seq": to},
            device_id_type=MESH,
        )

    def shard_of(piece, line, step):
        return held.at[piece, line, lax.rem(turn + step + RING, RING)]

    def half_of(piece, line, step, start):
        return held.at[piece, line, lax.rem(turn + step + RING, RING), pl.ds(start, half)]

    def right_copy(piece, line, step=0):
        return ring_copy(
            shard_of(piece, line, step), right, right_send.at[piece, line], right_recv.at[piece, line]
        )

    def left_copy(piece, line, step=0):
        return ring_copy(
            shard_of(piece, line, step), left, left_send.at[piece, line], left_recv.at[piece, line]
        )

    def far_right_copy(piece, line, step=-1):
        return ring_copy(
            half_of(piece, line, step, 0),
            right,
            far_right_send.at[piece, line],
            far_right_recv.at[piece, line],
        )

    def far_left_copy(piece, line, step=1):
        return ring_copy(
            half_of(piece, line, step, half),
            left,
            far_left_send.at[piece, line],
            far_left_recv.at[piece, line],
        )

    def along_ring(piece, line):
        right_copy(piece, line).start()
        left_copy(piece, line).start()

    def spread(piece):
        across_copy(piece).start()
        along_ring(piece, 0)

    def from_across(piece):
        across_copy(piece).wait_recv()
        along_ring(piece, 1)

    def farther(piece, line):
        right_copy(piece, line, -1).wait_recv()
        far_right_copy(piece, line).start()
        left_copy(piece, line, 1).wait_recv()
        far_left_copy(piece, line).start()

    def last_of(piece, line):
        far_right_copy(piece, line, -2).wait_recv()
        far_left_copy(piece, line, 2).wait_recv()

    def core_copy(unit):
        return pltpu.make_async_remote_copy(
            src_ref=part.at[unit, 1 - core],
            dst_ref=part_in.at[unit],
            send_sem=core_send.at[unit],
            recv_sem=core_recv.at[unit],
            device_id={"mp": 1 - core},
            device_id_type=MESH,
        )

    def section_copy(unit):
        line, owner = divmod(unit, 2)
        row = opposite_run if line else run
        return pltpu.make_async_remote_copy(
            src_ref=ready.at[unit],
            dst_ref=landed.at[row],
            send_sem=section_send.at[unit],
            recv_sem=section_recv.at[row],
            device_id={"section": back_section, "seq": paired if owner else seq_place},
            device_id_type=MESH,
        )

    def relay_copy():
        return pltpu.make_async_remote_copy(
            src_ref=ready.at[0],
            dst_ref=relayed,
            send_sem=section_send.at[0],
            recv_sem=relay_recv.at[0],
            device_id=at(first_column, ahead),
            device_id_type=MESH,
        )

    def forward_copy():
        return pltpu.make_async_remote_copy(
            src_ref=relayed,
            dst_ref=landed.at[opposite_run],
            send_sem=forward_send.at[0],
            recv_sem=section_recv.at[opposite_run],
            device_id=at(column, ahead),
            device_id_type=MESH,
        )

    def land(row):
        pltpu.make_async_remote_copy(
            src_ref=landed.at[row],
            dst_ref=landed.at[row],
            send_sem=forward_send.at[0],
            recv_sem=section_recv.at[row],
            device_id={"section": back_section},
            device_id_type=MESH,
        ).wait_recv()
        start = row * RING * rows
        out_ref[pl.ds(pl.multiple_of(start, RING * rows), RING * rows), :] = jnp.transpose(landed[row])

    def project(unit):
        line, owner = divmod(unit, 2)
        product = None
        for piece in range(PIECES):
            weight = weights_in[piece] if owner else weight_piece(piece)[...]
            shards = held[piece, line].reshape(RING * rows, -1)
            term = lax.dot_general(weight, shards, NT, preferred_element_type=jnp.float32)
            product = term if product is None else product + term
        part[unit, 0] = product[:width]
        part[unit, 1] = product[width:]
        core_copy(unit).start()

    def hand_over(unit):
        core_copy(unit).wait_recv()
        ready[unit] = (part[unit, core] + part_in[unit]).astype(jnp.bfloat16)
        if unit == 0:
            relay_copy().start()
        else:
            section_copy(unit).start()

    for head in range(heads):
        for kind in (0, 1):
            own_copy(kind, head).start()
        send_own(head)
        if head >= 1:
            send_relayed(head - 1)
    for piece in range(EARLY_WEIGHTS):
        weight_copy(piece).start()
    send_relayed(heads - 1)

    for step in range(1, RING + 1):

        @pl.when(seq_place < step)
        def _():
            for buffer in buffers:
                for head in range(heads):
                    buffer[head, slot(step)] = jnp.zeros((rows, HEAD_WIDTH), jnp.bfloat16)

    first_row = pl.multiple_of(seq_place * rows, rows)
    here = docs_ref[:, pl.ds(first_row, rows)].astype(jnp.float32)
    query_docs = jnp.transpose(jnp.broadcast_to(here, (rows, rows)))
    query_row = lax.broadcasted_iota(jnp.int32, (rows, rows), 0)
    key_row = lax.broadcasted_iota(jnp.int32, (rows, rows), 1)
    for step in range(RING + 1):
        start = pl.multiple_of(jnp.maximum(seq_place - step, 0) * rows, rows)
        there = docs_ref[:, pl.ds(start, rows)].astype(jnp.float32)
        offset = query_row - key_row + step * rows
        allowed = (query_docs == there) & (offset >= 0) & (offset < WINDOW)
        allowed = allowed & (jnp.full((rows, rows), seq_place, jnp.int32) >= step)
        bias[:, (RING - step) * rows : (RING - step + 1) * rows] = jnp.where(
            allowed, 0.0, -jnp.inf
        )

    for head in range(heads):
        wait_halo(head)
        attend(head)
        if head >= 1:
            collect_behind(head - 1)
        if head % 2:
            spread(head // 2)
    collect_behind(heads - 1)
    for piece in range(EARLY_WEIGHTS, PIECES):
        weight_copy(piece).start()
    farther(0, 0)
    from_across(0)
    for head in range(heads):
        collect_own(head)
    for piece in (2, 3):
        spread(piece)
    farther(1, 0)
    from_across(1)
    farther(0, 1)
    for piece in (2, 3):
        farther(piece, 0)
    for piece in range(PIECES):
        last_of(piece, 0)
    project(0)
    farther(1, 1)
    for piece in (2, 3):
        from_across(piece)
    hand_over(0)
    for piece in range(PIECES):
        weight_copy(piece).wait_recv()
    project(1)
    for piece in (2, 3):
        farther(piece, 1)
    hand_over(1)
    for piece in range(PIECES):
        last_of(piece, 1)
    project(2)
    project(3)
    hand_over(2)
    hand_over(3)
    relay_copy().wait_recv()
    forward_copy().start()
    for row in (lax.rem(run + 1, RING), opposite_run, lax.rem(run + 3, RING), run):
        land(row)

    for unit in range(4):
        core_copy(unit).wait_send()
        section_copy(unit).wait_send()
    forward_copy().wait_send()
    for piece in range(PIECES):
        weight_copy(piece).wait_send()
        across_copy(piece).wait_send()
        for line in (0, 1):
            right_copy(piece, line).wait_send()
            left_copy(piece, line).wait_send()
            far_right_copy(piece, line).wait_send()
            far_left_copy(piece, line).wait_send()
    for head in range(heads):
        for kind in (0, 1):
            for step in near:

                @pl.when((turn + step < RING) | (run > 0))
                def _():
                    halo_copy(kind, head, step, False).wait_send()

            @pl.when(run < RING - 1)
            def _():
                halo_copy(kind, head, RING, False).wait_send()

        for step in near:

            @pl.when(seq_place >= step)
            def _():
                back_copy(head, step).wait_send()

        @pl.when(run > 0)
        def _():
            line_copy(head).wait_send()


def cascade(docs, query, key, value, grad, w_query, key_weight, value_weight):
    rows = query.shape[0]
    heads = key.shape[1] // HEAD_WIDTH
    seq_count = lax.axis_size("seq")
    width = w_query.shape[0] // 2
    span = RING * rows
    cols = PIECE_HEADS * HEAD_WIDTH
    dma = pltpu.SemaphoreType.DMA
    whole = pl.BlockSpec(memory_space=pltpu.VMEM)
    tile = (rows, HEAD_WIDTH)
    return pl.pallas_call(
        cascade_kernel,
        out_shape=jax.ShapeDtypeStruct((seq_count * rows, width), jnp.bfloat16),
        in_specs=[whole] * 8,
        out_specs=whole,
        scratch_shapes=[
            pltpu.VMEM((heads, (RING + 1) * rows, HEAD_WIDTH), jnp.bfloat16),
            pltpu.VMEM((heads, (RING + 1) * rows, HEAD_WIDTH), jnp.bfloat16),
            pltpu.VMEM((rows, (RING + 1) * rows), jnp.float32),
            pltpu.VMEM((heads, 2, 2) + tile, jnp.float32),
            pltpu.VMEM((heads, RING - 1, 2) + tile, jnp.bfloat16),
            pltpu.VMEM((heads, RING - 1, 2) + tile, jnp.bfloat16),
            pltpu.VMEM((heads, 2) + tile, jnp.bfloat16),
            pltpu.VMEM((heads, 2) + tile, jnp.bfloat16),
            pltpu.VMEM((PIECES, 2, RING, rows, cols), jnp.bfloat16),
            pltpu.VMEM((PIECES, 2 * width, cols), jnp.bfloat16),
            pltpu.VMEM((4, 2, width, span), jnp.float32),
            pltpu.VMEM((4, width, span), jnp.float32),
            pltpu.VMEM((4, width, span), jnp.bfloat16),
            pltpu.VMEM((width, span), jnp.bfloat16),
            pltpu.VMEM((RING, width, span), jnp.bfloat16),
            dma((2, heads)),
            dma((2, RING, heads)),
            dma((2, RING, heads)),
            dma((heads, RING - 1)),
            dma((heads, RING - 1)),
            dma((heads,)),
            dma((heads,)),
            *([dma((PIECES,))] * 4),
            *([dma((PIECES, 2))] * 8),
            *([dma((4,))] * 4),
            *([dma((1,))] * 2),
        ],
        compiler_params=pltpu.CompilerParams(collective_id=0, has_side_effects=True),
    )(docs, query, key, value, grad, w_query, key_weight, value_weight)


def per_device(
    query_rows,
    key_row_matrix,
    value_row_matrix,
    out_grad,
    w_query,
    key_weight,
    value_weight,
    doc_ids,
):
    upstream = cascade(
        doc_ids,
        query_rows[0],
        key_row_matrix[0],
        value_row_matrix[0],
        out_grad[0],
        w_query[0],
        key_weight[0],
        value_weight[0],
    )
    return upstream[None]


def solution(mesh):
    placed = (
        P("section", "seq", "mp"),
        P("section", "seq", "mp"),
        P("section", "seq", "mp"),
        P("section", "seq", "mp"),
        P("section", "seq", "mp"),
        P("section", "seq", "mp"),
        P("section", "seq", "mp"),
        P("section", None),
    )
    return jax.shard_map(
        per_device,
        mesh=mesh,
        in_specs=placed,
        out_specs=P("section", None, ("seq", "mp")),
        check_vma=False,
    )
```

time: 167 us -> 126 us (0.75)
  the two profiles are of different devices: /device:TPU:1 before, /device:TPU:2 now
where the time goes in v3:
time: 126 us
  Pallas kernels  123 us (98%)
  local copies, waits for them, and re-layouts  2.16 us (2%)
    pallas_call x1, Pallas kernels, cascade(): pl.pallas_call(cascade_kernel, out_shape=jax.ShapeDtypeStruct((seq_count...  123 us

profile of v3, /device:TPU:2, one launch (start us, length us, event | category | flops | bytes accessed | tf_op | source)
XLA Modules:
  0.0 125.7 jit_solution(783259809651035109)
XLA Ops:
  0.0 123.5 %shard_map.82 = bf16[2048,168]{1,0:T(8,128)(2,1)} custom-call(s32[1,2048]{1,0:T(1,128)} %docs_ref.1, bf16[128,1024]{1,0:T(8,128)(2,1)} %bitcast.12, bf16[128,512]{1,0:T(8,128)(2,1)} %bitcast.14, bf16[128,512]{1,0:T(8,128)(2,1)} %bitcast.15, bf16[128,1024]{1,0:T(8,128)(2,1)} %bitcast.13, bf16[336,1024]{1,0:T(8,128)(2,1)} %bitcast.9, ...), custom_call_target="tpu_custom_call" | custom-call | tf_op jit(solution)/shard_map/pallas_call | solution.py:591
  123.5 2.2 %copy.9 = bf16[1,2048,168]{1,2,0:T(8,128)(2,1)} copy(bf16[1,2048,168]{2,1,0:T(8,128)(2,1)} %bitcast.8) | data formatting | bytes 1376256 | tf_op jit(solution)/shard_map/broadcast_in_dim | solution.py:648

commit v4 on v3

v4 whole, which is shorter than its diff:
```python
import math

import jax
import jax.numpy as jnp
from jax import lax
from jax.experimental import pallas as pl
from jax.experimental.pallas import tpu as pltpu
from jax.sharding import PartitionSpec as P

HEAD_WIDTH = 128
WINDOW = 512
RING = 4
LEG = 6
MESH = pl.DeviceIdType.MESH
NT = (((1,), (1,)), ((), ()))
TN = (((0,), (0,)), ((), ()))
PIECES = 2
EARLY_WEIGHTS = 2


def signal(semaphore, device):
    pl.semaphore_signal(semaphore, inc=1, device_id=device, device_id_type=MESH)


def cascade_kernel(
    docs_ref,
    query_ref,
    key_ref,
    value_ref,
    grad_ref,
    w_query_ref,
    key_weight_ref,
    value_weight_ref,
    out_ref,
    keys,
    values,
    queries,
    grads,
    bias,
    sums,
    behind,
    behind_in,
    weights,
    weights_in,
    held,
    part,
    part_in,
    ready,
    relayed,
    landed,
    own_sem,
    own_weight_sem,
    swap_send,
    swap_recv,
    halo_send,
    halo_recv,
    line_send,
    line_recv,
    weight_send,
    weight_recv,
    across_send,
    across_recv,
    right_send,
    right_recv,
    left_send,
    left_recv,
    far_right_send,
    far_right_recv,
    far_left_send,
    far_left_recv,
    core_send,
    core_recv,
    section_send,
    section_recv,
    relay_recv,
    forward_send,
):
    seq_place = lax.axis_index("seq")
    core = lax.axis_index("mp")
    section = lax.axis_index("section")
    section_count = lax.axis_size("section")
    run = seq_place // RING
    turn = lax.rem(seq_place, RING)
    column = section // RING
    block = lax.rem(section, RING)
    rows = query_ref.shape[0]
    span = RING * rows
    half = span // 2
    width = w_query_ref.shape[0] // 2
    scaling = 1.0 / math.sqrt(HEAD_WIDTH)
    near = range(1, RING)

    right = run * RING + lax.rem(turn + 1, RING)
    left = run * RING + lax.rem(turn + RING - 1, RING)
    paired_run = run + 1 - 2 * lax.rem(run, 2)
    paired = paired_run * RING + turn
    opposite_run = lax.rem(run + 2, RING)
    opposite = opposite_run * RING + turn
    back_section = lax.rem(section + section_count - 1, section_count)
    next_section = lax.rem(section + 1, section_count)

    depth = RING * RING
    along = block * RING + run
    ahead = lax.rem(along + LEG, depth)
    before = lax.rem(along + depth - LEG, depth)

    def at(col, place):
        return {"section": col * RING + place // RING, "seq": lax.rem(place, RING) * RING + turn}

    turned = block == 0
    from_turned = before < RING
    first_column = lax.rem(column + RING - turned.astype(jnp.int32), RING)
    source_column = lax.rem(column + from_turned.astype(jnp.int32), RING)

    barrier = pltpu.get_barrier_semaphore()
    for step in near:
        signal(barrier, {"seq": run * RING + lax.rem(turn + step, RING)})
    signal(barrier, {"seq": opposite})
    signal(barrier, {"mp": 1 - core})
    for place in (seq_place, paired):
        signal(barrier, {"section": back_section, "seq": place})
        signal(barrier, {"section": next_section, "seq": place})
    signal(barrier, at(column, ahead))
    signal(barrier, at(column, before))

    @pl.when(turned)
    def _():
        signal(barrier, at(first_column, ahead))

    @pl.when(from_turned)
    def _():
        signal(barrier, at(source_column, before))

    @pl.when(run < RING - 1)
    def _():
        signal(barrier, {"seq": seq_place + RING})

    @pl.when(run > 0)
    def _():
        signal(barrier, {"seq": seq_place - RING})

    peers = RING - 1 + 1 + 1 + 4 + 2
    peers = peers + turned.astype(jnp.int32) + from_turned.astype(jnp.int32)
    peers = peers + (run > 0).astype(jnp.int32) + (run < RING - 1).astype(jnp.int32)
    pl.semaphore_wait(barrier, peers)

    sources = (key_ref, value_ref, query_ref, grad_ref)
    buffers = (keys, values, queries, grads)

    def block_rows(place, first=0):
        return pl.ds(pl.multiple_of(first + place * rows, rows), rows)

    def head_cols(kind, head):
        wide = buffers[kind].shape[1]
        return sources[kind].at[:, pl.ds(pl.multiple_of(head * wide, HEAD_WIDTH), wide)]

    def home(kind):
        return span if kind < 2 else 0

    def own_copy(kind):
        return pltpu.make_async_copy(
            head_cols(kind, turn), buffers[kind].at[block_rows(turn, home(kind))], own_sem.at[kind]
        )

    def swap_copy(kind, step):
        to = lax.rem(turn + step, RING)
        return pltpu.make_async_remote_copy(
            src_ref=head_cols(kind, to),
            dst_ref=buffers[kind].at[block_rows(turn, home(kind))],
            send_sem=swap_send.at[kind, step - 1],
            recv_sem=swap_recv.at[kind, step - 1],
            device_id={"seq": run * RING + to},
            device_id_type=MESH,
        )

    def halo_copy(kind, step):
        place = lax.rem(turn + RING - step, RING)
        return pltpu.make_async_remote_copy(
            src_ref=buffers[kind].at[block_rows(place, span)] if step else head_cols(kind, turn),
            dst_ref=buffers[kind].at[block_rows(place)],
            send_sem=halo_send.at[kind, step],
            recv_sem=halo_recv.at[kind, step],
            device_id={"seq": seq_place + RING},
            device_id_type=MESH,
        )

    def line_copy(place):
        return pltpu.make_async_remote_copy(
            src_ref=behind.at[place],
            dst_ref=behind_in.at[place],
            send_sem=line_send.at[place],
            recv_sem=line_recv.at[place],
            device_id={"seq": seq_place - RING},
            device_id_type=MESH,
        )

    def own_weight_copies(head):
        wide = 2 * HEAD_WIDTH
        query_cols = pl.ds(head * wide, wide)
        kv_span = pl.ds(head * HEAD_WIDTH, HEAD_WIDTH)
        return [
            pltpu.make_async_copy(source, target, own_weight_sem.at[head, index])
            for index, (source, target) in enumerate(
                (
                    (w_query_ref.at[:, query_cols], weights.at[head, :, pl.ds(0, wide)]),
                    (key_weight_ref.at[:, kv_span], weights.at[head, :, pl.ds(wide, HEAD_WIDTH)]),
                    (
                        value_weight_ref.at[:, kv_span],
                        weights.at[head, :, pl.ds(wide + HEAD_WIDTH, HEAD_WIDTH)],
                    ),
                )
            )
        ]

    def weight_copy(head):
        return pltpu.make_async_remote_copy(
            src_ref=weights.at[head],
            dst_ref=weights_in.at[head],
            send_sem=weight_send.at[head],
            recv_sem=weight_recv.at[head],
            device_id={"seq": paired},
            device_id_type=MESH,
        )

    def both(ref, place):
        block = ref[place * rows : (place + 1) * rows]
        return jnp.concatenate([block[:, :HEAD_WIDTH], block[:, HEAD_WIDTH:]], axis=0)

    def attend(place):
        query = both(queries, place)
        grad = both(grads, place)
        reach = slice(place * rows, place * rows + span + rows)
        key = keys[reach]
        value = values[reach]
        scores = lax.dot_general(query, key, NT, preferred_element_type=jnp.float32)
        mask = jnp.concatenate([bias[place], bias[place]], axis=0)
        scores = scores * scaling + mask
        raised = jnp.exp(scores - jnp.max(scores, axis=1, keepdims=True))
        weights_full = raised * (1.0 / jnp.sum(raised, axis=1, keepdims=True))
        weights_half = weights_full.astype(jnp.bfloat16)
        attended = jnp.dot(weights_half, value, preferred_element_type=jnp.float32)
        delta = jnp.sum(grad.astype(jnp.float32) * attended, axis=1, keepdims=True)
        grad_weights = lax.dot_general(grad, value, NT, preferred_element_type=jnp.float32)
        grad_scores = (weights_full * (grad_weights - delta)).astype(jnp.bfloat16)
        grad_query = jnp.dot(grad_scores, key, preferred_element_type=jnp.float32) * scaling
        grad_query = grad_query.astype(jnp.bfloat16)
        here = slice(place * rows, (place + 1) * rows)
        held[0, 0, turn, here, :HEAD_WIDTH] = grad_query[:rows]
        held[0, 0, turn, here, HEAD_WIDTH:] = grad_query[rows:]
        terms = (
            lax.dot_general(grad_scores, query, TN, preferred_element_type=jnp.float32) * scaling,
            lax.dot_general(weights_half, grad, TN, preferred_element_type=jnp.float32),
        )
        for kind in (0, 1):
            if place == 0:
                sums[kind, reach] = terms[kind]
            else:
                sums[kind, place * rows : place * rows + span] += terms[kind][:span]
                sums[kind, place * rows + span : place * rows + span + rows] = terms[kind][span:]

        @pl.when(run > 0)
        def _():
            behind[place] = sums[:, here].astype(jnp.bfloat16)
            line_copy(place).start()

    def collect(place):
        @pl.when(run < RING - 1)
        def _():
            line_copy(place).wait_recv()
            there = slice(span + place * rows, span + (place + 1) * rows)
            sums[:, there] += behind_in[place].astype(jnp.float32)

    def across_copy(piece):
        return pltpu.make_async_remote_copy(
            src_ref=held.at[piece, 0, turn],
            dst_ref=held.at[piece, 1, turn],
            send_sem=across_send.at[piece],
            recv_sem=across_recv.at[piece],
            device_id={"seq": opposite},
            device_id_type=MESH,
        )

    def ring_copy(shard, to, send, recv):
        return pltpu.make_async_remote_copy(
            src_ref=shard,
            dst_ref=shard,
            send_sem=send,
            recv_sem=recv,
            device_id={"seq": to},
            device_id_type=MESH,
        )

    def shard_of(piece, line, step):
        return held.at[piece, line, lax.rem(turn + step + RING, RING)]

    def half_of(piece, line, step, start):
        return held.at[piece, line, lax.rem(turn + step + RING, RING), pl.ds(start, half)]

    def right_copy(piece, line, step=0):
        return ring_copy(
            shard_of(piece, line, step), right, right_send.at[piece, line], right_recv.at[piece, line]
        )

    def left_copy(piece, line, step=0):
        return ring_copy(
            shard_of(piece, line, step), left, left_send.at[piece, line], left_recv.at[piece, line]
        )

    def far_right_copy(piece, line, step=-1):
        return ring_copy(
            half_of(piece, line, step, 0),
            right,
            far_right_send.at[piece, line],
            far_right_recv.at[piece, line],
        )

    def far_left_copy(piece, line, step=1):
        return ring_copy(
            half_of(piece, line, step, half),
            left,
            far_left_send.at[piece, line],
            far_left_recv.at[piece, line],
        )

    def along_ring(piece, line):
        right_copy(piece, line).start()
        left_copy(piece, line).start()

    def spread(piece):
        across_copy(piece).start()
        along_ring(piece, 0)

    def from_across(piece):
        across_copy(piece).wait_recv()
        along_ring(piece, 1)

    def farther(piece, line):
        right_copy(piece, line, -1).wait_recv()
        far_right_copy(piece, line).start()
        left_copy(piece, line, 1).wait_recv()
        far_left_copy(piece, line).start()

    def last_of(piece, line):
        far_right_copy(piece, line, -2).wait_recv()
        far_left_copy(piece, line, 2).wait_recv()

    def core_copy(unit):
        return pltpu.make_async_remote_copy(
            src_ref=part.at[unit, 1 - core],
            dst_ref=part_in.at[unit],
            send_sem=core_send.at[unit],
            recv_sem=core_recv.at[unit],
            device_id={"mp": 1 - core},
            device_id_type=MESH,
        )

    def section_copy(unit):
        line, owner = divmod(unit, 2)
        row = opposite_run if line else run
        return pltpu.make_async_remote_copy(
            src_ref=ready.at[unit],
            dst_ref=landed.at[row],
            send_sem=section_send.at[unit],
            recv_sem=section_recv.at[row],
            device_id={"section": back_section, "seq": paired if owner else seq_place},
            device_id_type=MESH,
        )

    def relay_copy():
        return pltpu.make_async_remote_copy(
            src_ref=ready.at[0],
            dst_ref=relayed,
            send_sem=section_send.at[0],
            recv_sem=relay_recv.at[0],
            device_id=at(first_column, ahead),
            device_id_type=MESH,
        )

    def forward_copy():
        return pltpu.make_async_remote_copy(
            src_ref=relayed,
            dst_ref=landed.at[opposite_run],
            send_sem=forward_send.at[0],
            recv_sem=section_recv.at[opposite_run],
            device_id=at(column, ahead),
            device_id_type=MESH,
        )

    def land(row):
        pltpu.make_async_remote_copy(
            src_ref=landed.at[row],
            dst_ref=landed.at[row],
            send_sem=forward_send.at[0],
            recv_sem=section_recv.at[row],
            device_id={"section": back_section},
            device_id_type=MESH,
        ).wait_recv()
        out_ref[pl.ds(pl.multiple_of(row * span, span), span), :] = jnp.transpose(landed[row])

    def project(unit):
        line, owner = divmod(unit, 2)
        source = weights_in if owner else weights
        product = None
        for head in range(RING):
            for piece in range(PIECES):
                weight = source[head, :, piece * 2 * HEAD_WIDTH : (piece + 1) * 2 * HEAD_WIDTH]
                term = lax.dot_general(
                    weight, held[piece, line, head], NT, preferred_element_type=jnp.float32
                )
                product = term if product is None else product + term
        part[unit, 0] = product[:width]
        part[unit, 1] = product[width:]
        core_copy(unit).start()

    def hand_over(unit):
        core_copy(unit).wait_recv()
        ready[unit] = (part[unit, core] + part_in[unit]).astype(jnp.bfloat16)
        if unit == 0:
            relay_copy().start()
        else:
            section_copy(unit).start()

    order = (1, 3, 2)
    for step in order:
        for kind in (0, 1):
            swap_copy(kind, step).start()

    @pl.when(run < RING - 1)
    def _():
        for kind in (0, 1):
            halo_copy(kind, 0).start()

    for kind in range(4):
        own_copy(kind).start()
    for step in order:
        for kind in (2, 3):
            swap_copy(kind, step).start()
    for head in range(RING):
        for copy in own_weight_copies(head):
            copy.start()

    query_row = lax.broadcasted_iota(jnp.int32, (rows, rows), 0)
    key_row = lax.broadcasted_iota(jnp.int32, (rows, rows), 1)

    def block_docs(place):
        start = pl.multiple_of(jnp.maximum(place, 0) * rows, rows)
        return docs_ref[:, pl.ds(start, rows)].astype(jnp.float32)

    for place in range(RING):
        query_place = run * RING + place
        query_docs = jnp.transpose(jnp.broadcast_to(block_docs(query_place), (rows, rows)))
        for step in range(RING + 1):
            offset = query_row - key_row + step * rows
            allowed = (query_docs == block_docs(query_place - step)) & (offset >= 0)
            allowed = allowed & (offset < WINDOW)
            allowed = allowed & (jnp.full((rows, rows), query_place, jnp.int32) >= step)
            first = (RING - step) * rows
            bias[place, :, first : first + rows] = jnp.where(allowed, 0.0, -jnp.inf)

    @pl.when(run == 0)
    def _():
        for buffer in (keys, values):
            buffer[:span] = jnp.zeros((span, HEAD_WIDTH), jnp.bfloat16)

    for step in order:
        for kind in (0, 1):
            swap_copy(kind, step).wait_recv()

        @pl.when(run < RING - 1)
        def _():
            for kind in (0, 1):
                halo_copy(kind, step).start()

    for head in range(RING):
        for copy in own_weight_copies(head):
            copy.wait()
    for head in range(EARLY_WEIGHTS):
        weight_copy(head).start()
    for kind in range(4):
        own_copy(kind).wait()
    for step in order:
        for kind in (2, 3):
            swap_copy(kind, step).wait_recv()

    @pl.when(run > 0)
    def _():
        for step in range(RING):
            for kind in (0, 1):
                halo_copy(kind, step).wait_recv()

    for place in range(RING):
        attend(place)
    spread(0)
    for head in range(EARLY_WEIGHTS, RING):
        weight_copy(head).start()
    for place in range(RING):
        collect(place)
    for kind in (0, 1):
        first = kind * HEAD_WIDTH
        held[1, 0, turn, :, first : first + HEAD_WIDTH] = sums[kind, span:].astype(jnp.bfloat16)
    spread(1)
    farther(0, 0)
    from_across(0)
    farther(1, 0)
    for piece in range(PIECES):
        last_of(piece, 0)
    project(0)
    farther(0, 1)
    from_across(1)
    hand_over(0)
    for head in range(RING):
        weight_copy(head).wait_recv()
    project(1)
    farther(1, 1)
    hand_over(1)
    for piece in range(PIECES):
        last_of(piece, 1)
    project(2)
    project(3)
    hand_over(2)
    hand_over(3)
    relay_copy().wait_recv()
    forward_copy().start()
    for row in (lax.rem(run + 1, RING), opposite_run, lax.rem(run + 3, RING), run):
        land(row)

    for unit in range(4):
        core_copy(unit).wait_send()
        section_copy(unit).wait_send()
    forward_copy().wait_send()
    for piece in range(PIECES):
        across_copy(piece).wait_send()
        for line in (0, 1):
            right_copy(piece, line).wait_send()
            left_copy(piece, line).wait_send()
            far_right_copy(piece, line).wait_send()
            far_left_copy(piece, line).wait_send()
    for head in range(RING):
        weight_copy(head).wait_send()
    for kind in range(4):
        for step in near:
            swap_copy(kind, step).wait_send()

    @pl.when(run < RING - 1)
    def _():
        for kind in (0, 1):
            for step in range(RING):
                halo_copy(kind, step).wait_send()

    @pl.when(run > 0)
    def _():
        for place in range(RING):
            line_copy(place).wait_send()


def cascade(docs, query, key, value, grad, w_query, key_weight, value_weight):
    rows = query.shape[0]
    seq_count = lax.axis_size("seq")
    width = w_query.shape[0] // 2
    span = RING * rows
    wide = 2 * HEAD_WIDTH
    dma = pltpu.SemaphoreType.DMA
    whole = pl.BlockSpec(memory_space=pltpu.VMEM)
    stay = pl.BlockSpec(memory_space=pl.ANY)
    return pl.pallas_call(
        cascade_kernel,
        out_shape=jax.ShapeDtypeStruct((seq_count * rows, width), jnp.bfloat16),
        in_specs=[whole] + [stay] * 7,
        out_specs=whole,
        scratch_shapes=[
            pltpu.VMEM((2 * span, HEAD_WIDTH), jnp.bfloat16),
            pltpu.VMEM((2 * span, HEAD_WIDTH), jnp.bfloat16),
            pltpu.VMEM((span, wide), jnp.bfloat16),
            pltpu.VMEM((span, wide), jnp.bfloat16),
            pltpu.VMEM((RING, rows, span + rows), jnp.float32),
            pltpu.VMEM((2, 2 * span, HEAD_WIDTH), jnp.float32),
            pltpu.VMEM((RING, 2, rows, HEAD_WIDTH), jnp.bfloat16),
            pltpu.VMEM((RING, 2, rows, HEAD_WIDTH), jnp.bfloat16),
            pltpu.VMEM((RING, 2 * width, 2 * wide), jnp.bfloat16),
            pltpu.VMEM((RING, 2 * width, 2 * wide), jnp.bfloat16),
            pltpu.VMEM((PIECES, 2, RING, span, wide), jnp.bfloat16),
            pltpu.VMEM((4, 2, width, span), jnp.float32),
            pltpu.VMEM((4, width, span), jnp.float32),
            pltpu.VMEM((4, width, span), jnp.bfloat16),
            pltpu.VMEM((width, span), jnp.bfloat16),
            pltpu.VMEM((RING, width, span), jnp.bfloat16),
            dma((4,)),
            dma((RING, 3)),
            dma((4, RING - 1)),
            dma((4, RING - 1)),
            dma((2, RING)),
            dma((2, RING)),
            *([dma((RING,))] * 4),
            *([dma((PIECES,))] * 2),
            *([dma((PIECES, 2))] * 8),
            *([dma((4,))] * 4),
            *([dma((1,))] * 2),
        ],
        compiler_params=pltpu.CompilerParams(collective_id=0, has_side_effects=True),
    )(docs, query, key, value, grad, w_query, key_weight, value_weight)


def per_device(
    query_rows,
    key_row_matrix,
    value_row_matrix,
    out_grad,
    w_query,
    key_weight,
    value_weight,
    doc_ids,
):
    upstream = cascade(
        doc_ids,
        query_rows[0],
        key_row_matrix[0],
        value_row_matrix[0],
        out_grad[0],
        w_query[0],
        key_weight[0],
        value_weight[0],
    )
    return upstream[None]


def solution(mesh):
    placed = (
        P("section", "seq", "mp"),
        P("section", "seq", "mp"),
        P("section", "seq", "mp"),
        P("section", "seq", "mp"),
        P("section", "seq", "mp"),
        P("section", "seq", "mp"),
        P("section", "seq", "mp"),
        P("section", None),
    )
    return jax.shard_map(
        per_device,
        mesh=mesh,
        in_specs=placed,
        out_specs=P("section", None, ("seq", "mp")),
        check_vma=False,
    )
```

time: 126 us -> 128 us (1.016)
  the two profiles are of different devices: /device:TPU:2 before, /device:TPU:3 now
where the time goes in v4:
time: 128 us
  Pallas kernels  125 us (98%)
  local copies, waits for them, and re-layouts  2.16 us (2%)
    pallas_call x1, Pallas kernels, cascade(): pl.pallas_call(cascade_kernel, out_shape=jax.ShapeDtypeStruct((seq_count...  125 us

profile of v4, /device:TPU:3, one launch (start us, length us, event | category | flops | bytes accessed | tf_op | source)
XLA Modules:
  0.0 127.6 jit_solution(13321521853770543089)
XLA Ops:
  0.0 125.4 %shard_map.82 = bf16[2048,168]{1,0:T(8,128)(2,1)} custom-call(s32[1,2048]{1,0:T(1,128)} %docs_ref.1, bf16[128,1024]{1,0:T(8,128)(2,1)} %bitcast.12, bf16[128,512]{1,0:T(8,128)(2,1)} %bitcast.14, bf16[128,512]{1,0:T(8,128)(2,1)} %bitcast.15, bf16[128,1024]{1,0:T(8,128)(2,1)} %bitcast.13, bf16[336,1024]{1,0:T(8,128)(2,1)} %bitcast.9, ...), custom_call_target="tpu_custom_call" | custom-call | tf_op jit(solution)/shard_map/pallas_call | solution.py:565
  125.5 2.2 %copy.9 = bf16[1,2048,168]{1,2,0:T(8,128)(2,1)} copy(bf16[1,2048,168]{2,1,0:T(8,128)(2,1)} %bitcast.8) | data formatting | bytes 1376256 | tf_op jit(solution)/shard_map/broadcast_in_dim | solution.py:623

commit v5 on v4

--- a/solution.py
+++ b/solution.py
@@ -15,7 +15,8 @@
 NT = (((1,), (1,)), ((), ()))
 TN = (((0,), (0,)), ((), ()))
 PIECES = 2
-EARLY_WEIGHTS = 2
+EARLY_EVEN = 4
+EARLY_ODD = 2
 
 
 def signal(semaphore, device):
@@ -101,16 +102,17 @@
 
     depth = RING * RING
     along = block * RING + run
+    odd = lax.rem(run, 2) == 1
     ahead = lax.rem(along + LEG, depth)
     before = lax.rem(along + depth - LEG, depth)
+    after_relay = lax.rem(along + LEG - 1, depth)
+    before_relay = lax.rem(along + depth - LEG + 1, depth)
 
     def at(col, place):
         return {"section": col * RING + place // RING, "seq": lax.rem(place, RING) * RING + turn}
 
-    turned = block == 0
-    from_turned = before < RING
-    first_column = lax.rem(column + RING - turned.astype(jnp.int32), RING)
-    source_column = lax.rem(column + from_turned.astype(jnp.int32), RING)
+    first_column = lax.rem(column + RING - (block == 0).astype(jnp.int32), RING)
+    source_column = lax.rem(column + (before < RING).astype(jnp.int32), RING)
 
     barrier = pltpu.get_barrier_semaphore()
     for step in near:
@@ -120,16 +122,16 @@
     for place in (seq_place, paired):
         signal(barrier, {"section": back_section, "seq": place})
         signal(barrier, {"section": next_section, "seq": place})
-    signal(barrier, at(column, ahead))
-    signal(barrier, at(column, before))
-
-    @pl.when(turned)
+
+    @pl.when(odd)
     def _():
         signal(barrier, at(first_column, ahead))
-
-    @pl.when(from_turned)
-    def _():
         signal(barrier, at(source_column, before))
+        signal(barrier, at(column, after_relay))
+
+    @pl.when(jnp.logical_not(odd))
+    def _():
+        signal(barrier, at(column, before_relay))
 
     @pl.when(run < RING - 1)
     def _():
@@ -139,10 +141,8 @@
     def _():
         signal(barrier, {"seq": seq_place - RING})
 
-    peers = RING - 1 + 1 + 1 + 4 + 2
-    peers = peers + turned.astype(jnp.int32) + from_turned.astype(jnp.int32)
+    peers = RING - 1 + 1 + 1 + 4 + 1 + 2 * odd.astype(jnp.int32)
     peers = peers + (run > 0).astype(jnp.int32) + (run < RING - 1).astype(jnp.int32)
-    pl.semaphore_wait(barrier, peers)
 
     sources = (key_ref, value_ref, query_ref, grad_ref)
     buffers = (keys, values, queries, grads)
@@ -366,25 +366,32 @@
             device_id_type=MESH,
         )
 
-    def relay_copy():
-        return pltpu.make_async_remote_copy(
-            src_ref=ready.at[0],
-            dst_ref=relayed,
-            send_sem=section_send.at[0],
-            recv_sem=relay_recv.at[0],
+    def relay_copy(unit):
+        return pltpu.make_async_remote_copy(
+            src_ref=ready.at[unit],
+            dst_ref=relayed.at[unit // 2],
+            send_sem=section_send.at[unit],
+            recv_sem=relay_recv.at[unit // 2],
             device_id=at(first_column, ahead),
             device_id_type=MESH,
         )
 
-    def forward_copy():
-        return pltpu.make_async_remote_copy(
-            src_ref=relayed,
-            dst_ref=landed.at[opposite_run],
-            send_sem=forward_send.at[0],
-            recv_sem=section_recv.at[opposite_run],
-            device_id=at(column, ahead),
-            device_id_type=MESH,
-        )
+    def forward_copy(unit):
+        row = run if unit // 2 else opposite_run
+        return pltpu.make_async_remote_copy(
+            src_ref=relayed.at[unit // 2],
+            dst_ref=landed.at[row],
+            send_sem=forward_send.at[unit // 2],
+            recv_sem=section_recv.at[row],
+            device_id=at(column, after_relay),
+            device_id_type=MESH,
+        )
+
+    def forward(unit):
+        @pl.when(odd)
+        def _():
+            relay_copy(unit).wait_recv()
+            forward_copy(unit).start()
 
     def land(row):
         pltpu.make_async_remote_copy(
@@ -415,11 +422,24 @@
     def hand_over(unit):
         core_copy(unit).wait_recv()
         ready[unit] = (part[unit, core] + part_in[unit]).astype(jnp.bfloat16)
-        if unit == 0:
-            relay_copy().start()
+        if unit % 2 == 0:
+            section_copy(unit).start()
         else:
-            section_copy(unit).start()
-
+
+            @pl.when(odd)
+            def _():
+                relay_copy(unit).start()
+
+            @pl.when(jnp.logical_not(odd))
+            def _():
+                section_copy(unit).start()
+
+    for head in range(RING):
+        for copy in own_weight_copies(head):
+            copy.start()
+    for kind in range(4):
+        own_copy(kind).start()
+    pl.semaphore_wait(barrier, peers)
     order = (1, 3, 2)
     for step in order:
         for kind in (0, 1):
@@ -430,14 +450,16 @@
         for kind in (0, 1):
             halo_copy(kind, 0).start()
 
-    for kind in range(4):
-        own_copy(kind).start()
     for step in order:
         for kind in (2, 3):
             swap_copy(kind, step).start()
-    for head in range(RING):
-        for copy in own_weight_copies(head):
-            copy.start()
+
+    @pl.when(odd)
+    def _():
+        for head in range(EARLY_ODD):
+            for copy in own_weight_copies(head):
+                copy.wait()
+            weight_copy(head).start()
 
     query_row = lax.broadcasted_iota(jnp.int32, (rows, rows), 0)
     key_row = lax.broadcasted_iota(jnp.int32, (rows, rows), 1)
@@ -471,11 +493,13 @@
             for kind in (0, 1):
                 halo_copy(kind, step).start()
 
-    for head in range(RING):
-        for copy in own_weight_copies(head):
-            copy.wait()
-    for head in range(EARLY_WEIGHTS):
-        weight_copy(head).start()
+    @pl.when(jnp.logical_not(odd))
+    def _():
+        for head in range(EARLY_EVEN):
+            for copy in own_weight_copies(head):
+                copy.wait()
+            weight_copy(head).start()
+
     for kind in range(4):
         own_copy(kind).wait()
     for step in order:
@@ -491,14 +515,28 @@
     for place in range(RING):
         attend(place)
     spread(0)
-    for head in range(EARLY_WEIGHTS, RING):
-        weight_copy(head).start()
     for place in range(RING):
         collect(place)
     for kind in (0, 1):
         first = kind * HEAD_WIDTH
         held[1, 0, turn, :, first : first + HEAD_WIDTH] = sums[kind, span:].astype(jnp.bfloat16)
     spread(1)
+
+    @pl.when(odd)
+    def _():
+        for head in range(EARLY_ODD, RING):
+            for copy in own_weight_copies(head):
+                copy.wait()
+            weight_copy(head).start()
+
+    @pl.when(jnp.logical_not(odd))
+    def _():
+        for head in range(EARLY_EVEN, RING):
+            for copy in own_weight_copies(head):
+                copy.wait()
+            weight_copy(head).start()
+
+
     farther(0, 0)
     from_across(0)
     farther(1, 0)
@@ -516,18 +554,23 @@
     for piece in range(PIECES):
         last_of(piece, 1)
     project(2)
+    hand_over(2)
     project(3)
-    hand_over(2)
     hand_over(3)
-    relay_copy().wait_recv()
-    forward_copy().start()
-    for row in (lax.rem(run + 1, RING), opposite_run, lax.rem(run + 3, RING), run):
+    forward(1)
+    forward(3)
+    for row in (run, opposite_run, paired_run, lax.rem(paired_run + 2, RING)):
         land(row)
 
     for unit in range(4):
         core_copy(unit).wait_send()
         section_copy(unit).wait_send()
-    forward_copy().wait_send()
+
+    @pl.when(odd)
+    def _():
+        for unit in (1, 3):
+            forward_copy(unit).wait_send()
+
     for piece in range(PIECES):
         across_copy(piece).wait_send()
         for line in (0, 1):
@@ -582,7 +625,7 @@
             pltpu.VMEM((4, 2, width, span), jnp.float32),
             pltpu.VMEM((4, width, span), jnp.float32),
             pltpu.VMEM((4, width, span), jnp.bfloat16),
-            pltpu.VMEM((width, span), jnp.bfloat16),
+            pltpu.VMEM((2, width, span), jnp.bfloat16),
             pltpu.VMEM((RING, width, span), jnp.bfloat16),
             dma((4,)),
             dma((RING, 3)),
@@ -594,7 +637,7 @@
             *([dma((PIECES,))] * 2),
             *([dma((PIECES, 2))] * 8),
             *([dma((4,))] * 4),
-            *([dma((1,))] * 2),
+            *([dma((2,))] * 2),
         ],
         compiler_params=pltpu.CompilerParams(collective_id=0, has_side_effects=True),
     )(docs, query, key, value, grad, w_query, key_weight, value_weight)

time: 128 us -> 119 us (0.930)
  the two profiles are of different devices: /device:TPU:3 before, /device:TPU:1 now
where the time goes in v5:
time: 119 us; the launch traced here: 118 us
  Pallas kernels  116 us (97%)
  local copies, waits for them, and re-layouts  2.16 us (2%)
    pallas_call x1, Pallas kernels, cascade(): pl.pallas_call(cascade_kernel, out_shape=jax.ShapeDtypeStruct((seq_count...  116 us

profile of v5, /device:TPU:1, one launch (start us, length us, event | category | flops | bytes accessed | tf_op | source)
XLA Modules:
  0.0 118.3 jit_solution(15491522353494995107)
XLA Ops:
  0.0 116.2 %shard_map.82 = bf16[2048,168]{1,0:T(8,128)(2,1)} custom-call(s32[1,2048]{1,0:T(1,128)} %docs_ref.1, bf16[128,1024]{1,0:T(8,128)(2,1)} %bitcast.12, bf16[128,512]{1,0:T(8,128)(2,1)} %bitcast.14, bf16[128,512]{1,0:T(8,128)(2,1)} %bitcast.15, bf16[128,1024]{1,0:T(8,128)(2,1)} %bitcast.13, bf16[336,1024]{1,0:T(8,128)(2,1)} %bitcast.9, ...), custom_call_target="tpu_custom_call" | custom-call | tf_op jit(solution)/shard_map/pallas_call | solution.py:608
  116.2 2.2 %copy.9 = bf16[1,2048,168]{1,2,0:T(8,128)(2,1)} copy(bf16[1,2048,168]{2,1,0:T(8,128)(2,1)} %bitcast.8) | data formatting | bytes 1376256 | tf_op jit(solution)/shard_map/broadcast_in_dim | solution.py:666

commit v6 on v5

--- a/solution.py
+++ b/solution.py
@@ -366,6 +366,9 @@
             device_id_type=MESH,
         )
 
+    def goes_up(unit, origin):
+        return (origin == 3) | ((origin == 1) & (unit == 1))
+
     def relay_copy(unit):
         return pltpu.make_async_remote_copy(
             src_ref=ready.at[unit],
@@ -388,7 +391,7 @@
         )
 
     def forward(unit):
-        @pl.when(odd)
+        @pl.when(goes_up(unit, opposite_run))
         def _():
             relay_copy(unit).wait_recv()
             forward_copy(unit).start()
@@ -426,11 +429,11 @@
             section_copy(unit).start()
         else:
 
-            @pl.when(odd)
+            @pl.when(goes_up(unit, run))
             def _():
                 relay_copy(unit).start()
 
-            @pl.when(jnp.logical_not(odd))
+            @pl.when(jnp.logical_not(goes_up(unit, run)))
             def _():
                 section_copy(unit).start()
 
@@ -553,10 +556,10 @@
     hand_over(1)
     for piece in range(PIECES):
         last_of(piece, 1)
+    project(3)
     project(2)
+    hand_over(3)
     hand_over(2)
-    project(3)
-    hand_over(3)
     forward(1)
     forward(3)
     for row in (run, opposite_run, paired_run, lax.rem(paired_run + 2, RING)):
@@ -566,9 +569,10 @@
         core_copy(unit).wait_send()
         section_copy(unit).wait_send()
 
-    @pl.when(odd)
-    def _():
-        for unit in (1, 3):
+    for unit in (1, 3):
+
+        @pl.when(goes_up(unit, opposite_run))
+        def _():
             forward_copy(unit).wait_send()
 
     for piece in range(PIECES):

time: 119 us -> 116 us (0.975)
  the two profiles are of different devices: /device:TPU:1 before, /device:TPU:71 now
where the time goes in v6:
time: 116 us
  Pallas kernels  114 us (98%)
  local copies, waits for them, and re-layouts  2.16 us (2%)
    pallas_call x1, Pallas kernels, cascade(): pl.pallas_call(cascade_kernel, out_shape=jax.ShapeDtypeStruct((seq_count...  114 us

profile of v6, /device:TPU:71, one launch (start us, length us, event | category | flops | bytes accessed | tf_op | source)
XLA Modules:
  0.0 115.8 jit_solution(2707457673258533424)
XLA Ops:
  0.0 113.6 %shard_map.82 = bf16[2048,168]{1,0:T(8,128)(2,1)} custom-call(s32[1,2048]{1,0:T(1,128)} %docs_ref.1, bf16[128,1024]{1,0:T(8,128)(2,1)} %bitcast.12, bf16[128,512]{1,0:T(8,128)(2,1)} %bitcast.14, bf16[128,512]{1,0:T(8,128)(2,1)} %bitcast.15, bf16[128,1024]{1,0:T(8,128)(2,1)} %bitcast.13, bf16[336,1024]{1,0:T(8,128)(2,1)} %bitcast.9, ...), custom_call_target="tpu_custom_call" | custom-call | tf_op jit(solution)/shard_map/pallas_call | solution.py:612
  113.6 2.2 %copy.9 = bf16[1,2048,168]{1,2,0:T(8,128)(2,1)} copy(bf16[1,2048,168]{2,1,0:T(8,128)(2,1)} %bitcast.8) | data formatting | bytes 1376256 | tf_op jit(solution)/shard_map/broadcast_in_dim | solution.py:670

commit v7 on v6

--- a/solution.py
+++ b/solution.py
@@ -556,10 +556,10 @@
     hand_over(1)
     for piece in range(PIECES):
         last_of(piece, 1)
+    project(2)
+    hand_over(2)
     project(3)
-    project(2)
     hand_over(3)
-    hand_over(2)
     forward(1)
     forward(3)
     for row in (run, opposite_run, paired_run, lax.rem(paired_run + 2, RING)):

time: 116 us -> 114 us (0.983)
  the two profiles are of different devices: /device:TPU:71 before, /device:TPU:81 now
where the time goes in v7:
time: 114 us
  Pallas kernels  112 us (98%)
  local copies, waits for them, and re-layouts  2.16 us (2%)
    pallas_call x1, Pallas kernels, cascade(): pl.pallas_call(cascade_kernel, out_shape=jax.ShapeDtypeStruct((seq_count...  112 us

profile of v7, /device:TPU:81, one launch (start us, length us, event | category | flops | bytes accessed | tf_op | source)
XLA Modules:
  0.0 114.2 jit_solution(12086167538416741312)
XLA Ops:
  0.0 112.0 %shard_map.82 = bf16[2048,168]{1,0:T(8,128)(2,1)} custom-call(s32[1,2048]{1,0:T(1,128)} %docs_ref.1, bf16[128,1024]{1,0:T(8,128)(2,1)} %bitcast.12, bf16[128,512]{1,0:T(8,128)(2,1)} %bitcast.14, bf16[128,512]{1,0:T(8,128)(2,1)} %bitcast.15, bf16[128,1024]{1,0:T(8,128)(2,1)} %bitcast.13, bf16[336,1024]{1,0:T(8,128)(2,1)} %bitcast.9, ...), custom_call_target="tpu_custom_call" | custom-call | tf_op jit(solution)/shard_map/pallas_call | solution.py:612
  112.0 2.2 %copy.9 = bf16[1,2048,168]{1,2,0:T(8,128)(2,1)} copy(bf16[1,2048,168]{2,1,0:T(8,128)(2,1)} %bitcast.8) | data formatting | bytes 1376256 | tf_op jit(solution)/shard_map/broadcast_in_dim | solution.py:670

commit v8 on v7

--- a/solution.py
+++ b/solution.py
@@ -545,8 +545,8 @@
     farther(1, 0)
     for piece in range(PIECES):
         last_of(piece, 0)
+    farther(0, 1)
     project(0)
-    farther(0, 1)
     from_across(1)
     hand_over(0)
     for head in range(RING):

time: 114 us -> 114 us (level)
  the two profiles are of different devices: /device:TPU:81 before, /device:TPU:99 now
where the time goes in v8:
time: 114 us
  Pallas kernels  112 us (98%)
  local copies, waits for them, and re-layouts  2.16 us (2%)
    pallas_call x1, Pallas kernels, cascade(): pl.pallas_call(cascade_kernel, out_shape=jax.ShapeDtypeStruct((seq_count...  112 us

profile of v8, /device:TPU:99, one launch (start us, length us, event | category | flops | bytes accessed | tf_op | source)
XLA Modules:
  0.0 114.3 jit_solution(11296182642257755647)
XLA Ops:
  0.0 112.1 %shard_map.82 = bf16[2048,168]{1,0:T(8,128)(2,1)} custom-call(s32[1,2048]{1,0:T(1,128)} %docs_ref.1, bf16[128,1024]{1,0:T(8,128)(2,1)} %bitcast.12, bf16[128,512]{1,0:T(8,128)(2,1)} %bitcast.14, bf16[128,512]{1,0:T(8,128)(2,1)} %bitcast.15, bf16[128,1024]{1,0:T(8,128)(2,1)} %bitcast.13, bf16[336,1024]{1,0:T(8,128)(2,1)} %bitcast.9, ...), custom_call_target="tpu_custom_call" | custom-call | tf_op jit(solution)/shard_map/pallas_call | solution.py:612
  112.1 2.2 %copy.9 = bf16[1,2048,168]{1,2,0:T(8,128)(2,1)} copy(bf16[1,2048,168]{2,1,0:T(8,128)(2,1)} %bitcast.8) | data formatting | bytes 1376256 | tf_op jit(solution)/shard_map/broadcast_in_dim | solution.py:670

commit v9 on v7

--- a/solution.py
+++ b/solution.py
@@ -547,8 +547,8 @@
         last_of(piece, 0)
     project(0)
     farther(0, 1)
+    hand_over(0)
     from_across(1)
-    hand_over(0)
     for head in range(RING):
         weight_copy(head).wait_recv()
     project(1)

time: 114 us -> 114 us (level)
  the two profiles are of different devices: /device:TPU:81 before, /device:TPU:99 now
where the time goes in v9:
time: 114 us
  Pallas kernels  112 us (98%)
  local copies, waits for them, and re-layouts  2.16 us (2%)
    pallas_call x1, Pallas kernels, cascade(): pl.pallas_call(cascade_kernel, out_shape=jax.ShapeDtypeStruct((seq_count...  112 us

profile of v9, /device:TPU:99, one launch (start us, length us, event | category | flops | bytes accessed | tf_op | source)
XLA Modules:
  0.0 114.3 jit_solution(6350656534476906356)
XLA Ops:
  0.0 112.1 %shard_map.82 = bf16[2048,168]{1,0:T(8,128)(2,1)} custom-call(s32[1,2048]{1,0:T(1,128)} %docs_ref.1, bf16[128,1024]{1,0:T(8,128)(2,1)} %bitcast.12, bf16[128,512]{1,0:T(8,128)(2,1)} %bitcast.14, bf16[128,512]{1,0:T(8,128)(2,1)} %bitcast.15, bf16[128,1024]{1,0:T(8,128)(2,1)} %bitcast.13, bf16[336,1024]{1,0:T(8,128)(2,1)} %bitcast.9, ...), custom_call_target="tpu_custom_call" | custom-call | tf_op jit(solution)/shard_map/pallas_call | solution.py:612
  112.1 2.2 %copy.9 = bf16[1,2048,168]{1,2,0:T(8,128)(2,1)} copy(bf16[1,2048,168]{2,1,0:T(8,128)(2,1)} %bitcast.8) | data formatting | bytes 1376256 | tf_op jit(solution)/shard_map/broadcast_in_dim | solution.py:670
